TPU v7x, 512 devices: a whole 4x8x8 slice. The times are simulated.
512 devices in a mesh: dp: 4 (over x), expert: 128 (over z, y, core).
Axes of the slice: x: 4, y: 8, z: 8, core: 2. Of those that a mesh axis runs over, the one named last changes fastest.
Arguments:
- tokens: bfloat16 [8192, 2048], P(('dp', 'expert')), may hold values from -6 to 6
- routes: int32 [8192, 8], P(('dp', 'expert')), may hold values from 0 to 127, all different within a row; in each aligned block of 16 rows (0 to 15, 16 to 31, ...) at most 2 rows name the same one
- gates: float32 [8192, 8], P(('dp', 'expert')), may hold values from 0.02 to 0.5
- cotangent: bfloat16 [8192, 2048], P(('dp', 'expert')), may hold values from -6 to 6
- w_gate: bfloat16 [128, 2048, 768], P('expert', 'dp'), may hold values from -0.125 to 0.125
- w_up: bfloat16 [128, 2048, 768], P('expert', 'dp'), may hold values from -0.125 to 0.125
- w_down: bfloat16 [128, 768, 2048], P('expert', None, 'dp'), may hold values from -0.21875 to 0.21875
Outputs:
- layer_out: bfloat16 [8192, 2048], P(('dp', 'expert'))
- d_tokens: bfloat16 [8192, 2048], P(('dp', 'expert'))
- grad_gate: bfloat16 [128, 2048, 768], P('expert', 'dp')
- grad_up: bfloat16 [128, 2048, 768], P('expert', 'dp')
- grad_down: bfloat16 [128, 768, 2048], P('expert', None, 'dp')
Inputs may be any that keep to these rules, and one draw needn't show every extreme that they name: `routes`: each token names 8 different experts. Among the 16 tokens of one device (aligned blocks of token rows) no expert is named by more than 2 tokens, a bound that some block reaches.
All inputs are finite; a program needn't handle non-finite values.
Results may differ from a plain program's by a relative error of at most 0.019.
Values may be sent and summed in bfloat16 or wider, within the bound.
A program may use at most 64 MiB of HBM per device.

v0:
```python
import jax
import jax.numpy as jnp
from jax import lax
from jax.sharding import PartitionSpec as P


def local(tokens, routes, gates, cotangent, w_gate, w_up, w_down):
    tok_rows, features = tokens.shape
    fanout = routes.shape[1]
    experts = lax.axis_size("expert")
    groups = lax.axis_size("dp")
    capacity = min(tok_rows, max(2, 2 * tok_rows * fanout // experts))
    assigned = tok_rows * fanout
    expert_ids = routes.reshape(assigned)
    onehot = (expert_ids[:, None] == jnp.arange(experts, dtype=jnp.int32)[None, :]).astype(
        jnp.float32
    )
    assign_iota = jnp.arange(assigned, dtype=jnp.int32)
    earlier = (assign_iota[:, None] > assign_iota[None, :]).astype(jnp.float32)
    prior_count = jnp.dot(earlier, onehot, precision=lax.Precision.HIGHEST)
    slot_index = jnp.sum(prior_count * onehot, axis=1).astype(jnp.int32)
    position = expert_ids * capacity + slot_index
    slot_map = (
        jnp.arange(experts * capacity, dtype=jnp.int32)[:, None] == position[None, :]
    ).astype(jnp.float32)
    token_owner = (
        assign_iota[:, None] // fanout == jnp.arange(tok_rows, dtype=jnp.int32)[None, :]
    ).astype(jnp.float32)
    dispatch = jnp.dot(slot_map, token_owner, precision=lax.Precision.HIGHEST)
    weighted = jnp.dot(
        slot_map, token_owner * gates.reshape(assigned)[:, None], precision=lax.Precision.HIGHEST
    )
    send_input = jnp.dot(
        dispatch.astype(jnp.bfloat16), tokens, preferred_element_type=jnp.float32
    ).astype(jnp.bfloat16)
    send_dout = jnp.dot(
        weighted, cotangent.astype(jnp.float32), precision=lax.Precision.HIGHEST
    ).astype(jnp.bfloat16)
    send_input = send_input.reshape(1, experts, capacity, features)
    send_dout = send_dout.reshape(1, experts, capacity, features)
    moved = (
        lax.all_to_all(send_input, "expert", split_axis=1, concat_axis=1, tiled=True),
        lax.all_to_all(send_dout, "expert", split_axis=1, concat_axis=1, tiled=True),
    )
    moved = (
        lax.all_to_all(moved[0], "dp", split_axis=3, concat_axis=0, tiled=True),
        lax.all_to_all(moved[1], "dp", split_axis=3, concat_axis=0, tiled=True),
    )
    part_width = moved[0].shape[3]
    total_rows = groups * experts * capacity
    input_rows = moved[0].reshape(total_rows, part_width)
    dout_rows = moved[1].reshape(total_rows, part_width)
    gate_local = w_gate[0]
    up_local = w_up[0]
    down_local = w_down[0]
    own_rows = total_rows // groups
    own_start = lax.axis_index("dp") * own_rows
    gate_part = jnp.dot(input_rows, gate_local, preferred_element_type=jnp.float32)
    up_part = jnp.dot(input_rows, up_local, preferred_element_type=jnp.float32)
    gate_all, up_all = (
        lax.psum(gate_part.astype(jnp.bfloat16), "dp").astype(jnp.float32),
        lax.psum(up_part.astype(jnp.bfloat16), "dp").astype(jnp.float32),
    )
    hidden = (jax.nn.silu(gate_all) * up_all).astype(jnp.bfloat16)
    gate_own = lax.dynamic_slice_in_dim(gate_all, own_start, own_rows, 0)
    up_own = lax.dynamic_slice_in_dim(up_all, own_start, own_rows, 0)
    out_slots = jnp.dot(hidden, down_local, preferred_element_type=jnp.float32).astype(jnp.bfloat16)
    grad_down = jnp.einsum(
        "rf,rd->fd", hidden, dout_rows, preferred_element_type=jnp.float32
    ).astype(jnp.bfloat16)
    dhidden_part = jnp.einsum(
        "rd,fd->rf", dout_rows, down_local, preferred_element_type=jnp.float32
    )
    dhidden_own = lax.psum_scatter(
        dhidden_part.astype(jnp.bfloat16), "dp", scatter_dimension=0, tiled=True
    ).astype(jnp.float32)
    sigmoid_gate = jax.nn.sigmoid(gate_own)
    silu_gate = gate_own * sigmoid_gate
    dgate_own = (
        dhidden_own * up_own * sigmoid_gate * (1.0 + gate_own * (1.0 - sigmoid_gate))
    ).astype(jnp.bfloat16)
    dup_own = (dhidden_own * silu_gate).astype(jnp.bfloat16)
    dgate_all, dup_all = (
        lax.all_gather(dgate_own, "dp", axis=0, tiled=True),
        lax.all_gather(dup_own, "dp", axis=0, tiled=True),
    )
    grad_gate = jnp.einsum(
        "rd,rf->df", input_rows, dgate_all, preferred_element_type=jnp.float32
    ).astype(jnp.bfloat16)
    grad_up = jnp.einsum(
        "rd,rf->df", input_rows, dup_all, preferred_element_type=jnp.float32
    ).astype(jnp.bfloat16)
    back_slots = (
        jnp.einsum("rf,df->rd", dgate_all, gate_local, preferred_element_type=jnp.float32)
        + jnp.einsum("rf,df->rd", dup_all, up_local, preferred_element_type=jnp.float32)
    ).astype(jnp.bfloat16)
    out_slots = out_slots.reshape(groups, experts, capacity, part_width)
    back_slots = back_slots.reshape(groups, experts, capacity, part_width)
    returned = (
        lax.all_to_all(out_slots, "dp", split_axis=0, concat_axis=3, tiled=True),
        lax.all_to_all(back_slots, "dp", split_axis=0, concat_axis=3, tiled=True),
    )
    returned = (
        lax.all_to_all(returned[0], "expert", split_axis=1, concat_axis=1, tiled=True),
        lax.all_to_all(returned[1], "expert", split_axis=1, concat_axis=1, tiled=True),
    )
    out_tokens = returned[0].reshape(experts * capacity, features)
    back_tokens = returned[1].reshape(experts * capacity, features)
    layer_out = jnp.dot(
        weighted.T, out_tokens.astype(jnp.float32), precision=lax.Precision.HIGHEST
    ).astype(jnp.bfloat16)
    d_tokens = jnp.dot(
        dispatch.T.astype(jnp.bfloat16), back_tokens, preferred_element_type=jnp.float32
    ).astype(jnp.bfloat16)
    return (layer_out, d_tokens, grad_gate[None], grad_up[None], grad_down[None])


def solution(mesh):
    return jax.shard_map(
        local,
        mesh=mesh,
        in_specs=(
            P(("dp", "expert"), None),
            P(("dp", "expert"), None),
            P(("dp", "expert"), None),
            P(("dp", "expert"), None),
            P("expert", "dp", None),
            P("expert", "dp", None),
            P("expert", None, "dp"),
        ),
        out_specs=(
            P(("dp", "expert"), None),
            P(("dp", "expert"), None),
            P("expert", "dp", None),
            P("expert", "dp", None),
            P("expert", None, "dp"),
        ),
        check_vma=False,
    )
```

profile of v0, /device:TPU:1, one launch (start us, length us, event | category | flops | bytes accessed | tf_op | source)
XLA Modules:
  0.0 422.7 jit_solution(1155957234084271294)
XLA Ops:
  10.6 49.2 %all_to_all.86 = bf16[1,128,2,2048]{3,2,0,1:T(2,128)(2,1)S(1)} all-to-all(bf16[1,128,2,2048]{3,2,0,1:T(2,128)(2,1)S(1)} %bitcast.67), channel_id=1, replica_groups=mesh['dp'=4,'expert'=128] {'expert'}, dimensions={1} | all-to-all | bytes 2097152 | tf_op jit(solution)/shard_map/all_to_all | solution.py:42
  62.8 4.1 all-to-all-start.1
  70.0 11.8 %all-to-all-done.1 = bf16[1,128,2,2048]{1,2,0,3:T(2,128)(2,1)S(1)} async-done(((bf16[1,128,2,2048]{1,2,0,3:T(2,128)(2,1)}), bf16[1,128,2,2048]{1,2,0,3:T(2,128)(2,1)S(1)}, u32[]{:S(2)}, u32[]{:S(2)}) %all-to-all-start.1) | async-done | bytes 1048608 | tf_op jit(solution)/shard_map/all_to_all | solution.py:46
  81.7 7.1 %all-to-all-start.4 = ((bf16[1,128,2,2048]{3,2,0,1:T(2,128)(2,1)}), bf16[1,128,2,2048]{3,2,0,1:T(2,128)(2,1)S(1)}, u32[]{:S(2)}, u32[]{:S(2)}) async-start(bf16[1,128,2,2048]{3,2,0,1:T(2,128)(2,1)} %bitcast.9), calls=%async_computation.4 | async-start | bytes 2097152 | tf_op jit(solution)/shard_map/all_to_all | solution.py:43
  93.8 3.8 convolution_convert_fusion.5
  99.8 20.0 %all-to-all-done.4 = bf16[1,128,2,2048]{3,2,0,1:T(2,128)(2,1)S(1)} async-done(((bf16[1,128,2,2048]{3,2,0,1:T(2,128)(2,1)}), bf16[1,128,2,2048]{3,2,0,1:T(2,128)(2,1)S(1)}, u32[]{:S(2)}, u32[]{:S(2)}) %all-to-all-start.4) | async-done | bytes 1048608 | tf_op jit(solution)/shard_map/all_to_all | solution.py:43
  122.9 29.1 %all_to_all.87 = bf16[1,128,2,2048]{1,2,0,3:T(2,128)(2,1)S(1)} all-to-all(bf16[1,128,2,2048]{1,2,0,3:T(2,128)(2,1)S(1)} %copy.38), channel_id=1, replica_groups=mesh['dp'=4,'expert'=128] {'dp'}, dimensions={3} | all-to-all | bytes 2097152 | tf_op jit(solution)/shard_map/all_to_all | solution.py:47
  155.8 40.5 %all-reduce.3.cloned.1.call-done = (bf16[1024,768]{1,0:T(8,128)(2,1)}, bf16[1024,768]{1,0:T(8,128)(2,1)}) async-done(((bf16[1024,768]{1,0:T(8,128)(2,1)}, bf16[1024,768]{1,0:T(8,128)(2,1)}), (bf16[1024,768]{1,0:T(8,128)(2,1)}, bf16[1024,768]{1,0:T(8,128)(2,1)})) %all-reduce.3.cloned.1.call-update) | async-done | bytes 3145744 | tf_op jit(solution)/shard_map/psum | solution.py:62
  196.3 3.4 convert_element_type.76
  201.7 27.7 %reduce-scatter.2.cloned.1.call-done = bf16[256,768]{1,0:T(8,128)(2,1)} async-done(((bf16[1024,768]{1,0:T(8,128)(2,1)}), bf16[256,768]{1,0:T(8,128)(2,1)}) %reduce-scatter.2.cloned.1.call-update) | async-done | bytes 393232 | tf_op jit(solution)/shard_map/reduce_scatter | solution.py:74
  239.8 3.6 all-to-all-start.2
  243.4 28.2 %all-gather.3.cloned.1.call-done = bf16[1024,768]{1,0:T(8,128)(2,1)} async-done(((bf16[256,768]{1,0:T(8,128)(2,1)}), bf16[1024,768]{1,0:T(8,128)(2,1)}) %all-gather.3.cloned.1.call-update) | async-done | bytes 1572880 | tf_op jit(solution)/shard_map/all_gather | solution.py:84
  271.6 3.8 fusion.12
  275.4 30.0 %all-gather.5.cloned.1.call-done = bf16[1024,768]{1,0:T(8,128)(2,1)} async-done(((bf16[256,768]{1,0:T(8,128)(2,1)}), bf16[1024,768]{1,0:T(8,128)(2,1)}) %all-gather.5.cloned.1.call-update) | async-done | bytes 1572880 | tf_op jit(solution)/shard_map/all_gather | solution.py:85
  305.4 4.4 %add_convert_fusion = bf16[1024,512]{1,0:T(8,128)(2,1)} fusion(f32[1024,512]{1,0:T(8,128)} %fusion.12, bf16[1024,768]{1,0:T(8,128)(2,1)} %all-gather.5.cloned.1.call-done, bf16[1,512,768]{2,1,0:T(8,128)(2,1)} %param.12), kind=kOutput, calls=%fused_computation.5 | convolution fusion | flops 806354944 | bytes 5505024 | tf_op jit(solution)/shard_map/rf,df->rd/dot_general | solution.py:95
  313.3 3.5 all-to-all-start.6
  317.9 3.7 copy.36
  321.7 9.5 %all-to-all-done.6 = bf16[4,128,2,512]{1,3,2,0:T(8,128)(2,1)S(1)} async-done(((bf16[4,128,2,512]{1,3,2,0:T(8,128)(2,1)}), bf16[4,128,2,512]{1,3,2,0:T(8,128)(2,1)S(1)}, u32[]{:S(2)}, u32[]{:S(2)}) %all-to-all-start.6) | async-done | bytes 1048608 | tf_op jit(solution)/shard_map/all_to_all | solution.py:101
  331.2 15.3 %all-to-all-start.3 = ((bf16[1,128,2,2048]{3,2,0,1:T(2,128)(2,1)}), bf16[1,128,2,2048]{3,2,0,1:T(2,128)(2,1)S(1)}, u32[]{:S(2)}, u32[]{:S(2)}) async-start(bf16[1,128,2,2048]{3,2,0,1:T(2,128)(2,1)} %copy.36), calls=%async_computation.3 | async-start | bytes 2097152 | tf_op jit(solution)/shard_map/all_to_all | solution.py:104
  347.6 3.7 copy.43
  351.3 26.2 %all-to-all-done.3 = bf16[1,128,2,2048]{3,2,0,1:T(2,128)(2,1)S(1)} async-done(((bf16[1,128,2,2048]{3,2,0,1:T(2,128)(2,1)}), bf16[1,128,2,2048]{3,2,0,1:T(2,128)(2,1)S(1)}, u32[]{:S(2)}, u32[]{:S(2)}) %all-to-all-start.3) | async-done | bytes 1048608 | tf_op jit(solution)/shard_map/all_to_all | solution.py:104
  377.5 6.4 %all-to-all-start.7 = ((bf16[1,128,2,2048]{3,2,0,1:T(2,128)(2,1)}), bf16[1,128,2,2048]{3,2,0,1:T(2,128)(2,1)S(1)}, u32[]{:S(2)}, u32[]{:S(2)}) async-start(bf16[1,128,2,2048]{3,2,0,1:T(2,128)(2,1)} %copy.43), calls=%async_computation.8 | async-start | bytes 2097152 | tf_op jit(solution)/shard_map/all_to_all | solution.py:105
  383.9 3.7 fusion.2
  395.1 19.8 %all-to-all-done.7 = bf16[1,128,2,2048]{3,2,0,1:T(2,128)(2,1)S(1)} async-done(((bf16[1,128,2,2048]{3,2,0,1:T(2,128)(2,1)}), bf16[1,128,2,2048]{3,2,0,1:T(2,128)(2,1)S(1)}, u32[]{:S(2)}, u32[]{:S(2)}) %all-to-all-start.7) | async-done | bytes 1048608 | tf_op jit(solution)/shard_map/all_to_all | solution.py:105
  (71 shorter events, 50.1 us)
Async XLA Ops:
  7.2 146.3 %copy-start = (bf16[1,768,512]{2,1,0:T(8,128)(2,1)S(1)}, bf16[1,768,512]{2,1,0:T(8,128)(2,1)}, u32[]{:S(2)}) copy-start(bf16[1,768,512]{2,1,0:T(8,128)(2,1)} %param.13) | copy-start | bytes 2359300
  59.7 7.2 %copy-start.7 = (f32[16,8]{0,1:T(8,128)S(1)}, f32[16,8]{0,1:T(8,128)}, u32[]{:S(2)}) copy-start(f32[16,8]{0,1:T(8,128)} %param.9) | copy-start | bytes 1540
  62.8 4.6 %copy-start.6 = (bf16[16,2048]{1,0:T(8,128)(2,1)S(1)}, bf16[16,2048]{1,0:T(8,128)(2,1)}, u32[]{:S(2)}) copy-start(bf16[16,2048]{1,0:T(8,128)(2,1)} %param.10) | copy-start | bytes 196612
  62.8 18.9 %all-to-all-start.1 = ((bf16[1,128,2,2048]{1,2,0,3:T(2,128)(2,1)}), bf16[1,128,2,2048]{1,2,0,3:T(2,128)(2,1)S(1)}, u32[]{:S(2)}, u32[]{:S(2)}) async-start(bf16[1,128,2,2048]{1,2,0,3:T(2,128)(2,1)} %copy.31), calls=%async_computation.1 | async-start | bytes 2097152 | tf_op jit(solution)/shard_map/all_to_all | solution.py:46
  81.7 38.0 %all-to-all-start.4 = ((bf16[1,128,2,2048]{3,2,0,1:T(2,128)(2,1)}), bf16[1,128,2,2048]{3,2,0,1:T(2,128)(2,1)S(1)}, u32[]{:S(2)}, u32[]{:S(2)}) async-start(bf16[1,128,2,2048]{3,2,0,1:T(2,128)(2,1)} %bitcast.9), calls=%async_computation.4 | async-start | bytes 2097152 | tf_op jit(solution)/shard_map/all_to_all | solution.py:43
  88.8 107.5 %all-reduce.3.cloned.1.call-start = ((), (), s32[]{:S(2)}) async-start(), calls=%async_computation.12 | async-start | bytes 6291456 | tf_op jit(solution)/shard_map/psum | solution.py:62
  93.8 3.8 copy-start.3
  93.8 3.8 copy-start.10
  99.7 129.7 %reduce-scatter.2.cloned.1.call-start = ((), (), s32[]{:S(2)}) async-start(), calls=%async_computation.9 | async-start | bytes 1966080 | tf_op jit(solution)/shard_map/reduce_scatter | solution.py:74
  153.5 2.3 copy-start.5
  155.8 115.9 %all-gather.3.cloned.1.call-start = ((), (), s32[]{:S(2)}) async-start(), calls=%async_computation.10 | async-start | bytes 1966080 | tf_op jit(solution)/shard_map/all_gather | solution.py:84
  196.3 3.4 copy-start.1
  232.2 73.2 %all-gather.5.cloned.1.call-start = ((), (), s32[]{:S(2)}) async-start(), calls=%async_computation.11 | async-start | bytes 1966080 | tf_op jit(solution)/shard_map/all_gather | solution.py:85
  235.1 1.2 copy-start.2
  239.8 31.9 %copy-start.11 = (bf16[1,512,768]{2,1,0:T(8,128)(2,1)S(1)}, bf16[1,512,768]{2,1,0:T(8,128)(2,1)}, u32[]{:S(2)}) copy-start(bf16[1,512,768]{2,1,0:T(8,128)(2,1)} %param.11) | copy-start | bytes 2359300
  239.8 73.6 %all-to-all-start.2 = ((bf16[4,128,2,512]{1,3,2,0:T(8,128)(2,1)}), bf16[4,128,2,512]{1,3,2,0:T(8,128)(2,1)S(1)}, u32[]{:S(2)}, u32[]{:S(2)}) async-start(bf16[4,128,2,512]{1,3,2,0:T(8,128)(2,1)} %copy.34), calls=%async_computation.2 | async-start | bytes 2097152 | tf_op jit(solution)/shard_map/all_to_all | solution.py:100
  313.3 17.8 %all-to-all-start.6 = ((bf16[4,128,2,512]{1,3,2,0:T(8,128)(2,1)}), bf16[4,128,2,512]{1,3,2,0:T(8,128)(2,1)S(1)}, u32[]{:S(2)}, u32[]{:S(2)}) async-start(bf16[4,128,2,512]{1,3,2,0:T(8,128)(2,1)} %copy.41), calls=%async_computation.7 | async-start | bytes 2097152 | tf_op jit(solution)/shard_map/all_to_all | solution.py:101
  331.2 46.3 %all-to-all-start.3 = ((bf16[1,128,2,2048]{3,2,0,1:T(2,128)(2,1)}), bf16[1,128,2,2048]{3,2,0,1:T(2,128)(2,1)S(1)}, u32[]{:S(2)}, u32[]{:S(2)}) async-start(bf16[1,128,2,2048]{3,2,0,1:T(2,128)(2,1)} %copy.36), calls=%async_computation.3 | async-start | bytes 2097152 | tf_op jit(solution)/shard_map/all_to_all | solution.py:104
  377.5 37.4 %all-to-all-start.7 = ((bf16[1,128,2,2048]{3,2,0,1:T(2,128)(2,1)}), bf16[1,128,2,2048]{3,2,0,1:T(2,128)(2,1)S(1)}, u32[]{:S(2)}, u32[]{:S(2)}) async-start(bf16[1,128,2,2048]{3,2,0,1:T(2,128)(2,1)} %copy.43), calls=%async_computation.8 | async-start | bytes 2097152 | tf_op jit(solution)/shard_map/all_to_all | solution.py:105
  383.9 3.8 copy-start.4
  383.9 3.8 copy-start.8
  387.7 1.9 copy-start.9
Sparse Core Ops, SparseCore 0:
  99.9 96.4 all-reduce.2
  199.2 30.1 reduce-scatter.1
  232.3 39.2 all-gather.2
  274.2 31.2 all-gather.4
where the time goes:
time: 424 us; the launch traced here: 423 us
  waiting for transfers between devices  214 us (50%)
  blocking collectives  78.3 us (18%)
  starting transfers between devices  40.5 us (10%)
  local copies, waits for them, and re-layouts  34.2 us (8%)
  matrix products  31.2 us (7%)
  between operations  14 us (3%)
  other arithmetic  10.5 us (2%)
    all_to_all x1, blocking collectives, local(): lax.all_to_all(send_input, 'expert', split_axis=1, concat_axis=1, tiled=T...  49.2 us
    psum x1, waiting for transfers between devices, local(): lax.psum(up_part.astype(jnp.bfloat16), 'dp').astype(jnp.float32)  40.5 us
    all_gather x1, waiting for transfers between devices, local(): lax.all_gather(dup_own, 'dp', axis=0, tiled=True)  30 us
    all_to_all x1, blocking collectives, local(): lax.all_to_all(moved[1], 'dp', split_axis=3, concat_axis=0, tiled=True)  29.1 us
    all_gather x1, waiting for transfers between devices, local(): lax.all_gather(dgate_own, 'dp', axis=0, tiled=True)  28.2 us
    reduce_scatter x1, waiting for transfers between devices, local(): lax.psum_scatter(dhidden_part.astype(jnp.bfloat16), 'dp', scatter_dimensi...  27.7 us
    all_to_all x1, waiting for transfers between devices, local(): lax.all_to_all(returned[0], 'expert', split_axis=1, concat_axis=1, tiled=...  26.2 us
    all_to_all x1, waiting for transfers between devices, local(): lax.all_to_all(send_dout, 'expert', split_axis=1, concat_axis=1, tiled=True)  20 us
  transfers between devices with their start and end apart: 10, of which 9 were waited for; matrix products, arithmetic and copies ran while one was open for 15% of the time, Pallas kernels for 0%

commit v1 on v0

v1 whole, which is shorter than its diff:
```python
import functools

import jax
import jax.numpy as jnp
from jax import lax
from jax.experimental import pallas as pl
from jax.experimental.pallas import tpu as pltpu
from jax.sharding import PartitionSpec as P

MESH = pl.DeviceIdType.MESH
LAYOUT = {128: (8, 8, 2), 4: (2, 2, 1), 8: (2, 2, 2)}
F32, BF16 = jnp.float32, jnp.bfloat16


def fit(total, want):
    return want if total % want == 0 else total


class Sems:
    def __init__(self):
        self.count = 0

    def take(self, n):
        first = self.count
        self.count += n
        return first


def body(
    cfg,
    routes_ref, gates_ref, tok_ref, cot_ref, wg_hbm, wu_hbm, wd_hbm,
    out_ref, dtok_ref, gg_ref, gu_ref, gd_ref,
    wgu, wd, xinfo, xdata, ginfo, gdata, dmat, whi, wlo, gcol,
    rows, recv, pgu, pdh, rgu, rdh, hid, dgu, gate_s, gacc, gdacc,
    ret_s, ret, part, psum, fin, land,
    wsem, ssem, rsem,
):
    nz, ny, nc, dq, ff, tok = cfg
    xs = 4
    i = lax.axis_index("dp")
    e = lax.axis_index("expert")
    z, yc = e // (ny * nc), e % (ny * nc)
    y, c = yc // nc, yc % nc
    zc = z * nc + c
    right, left, opp = (i + 1) % xs, (i + 3) % xs, (i + 2) % xs
    sems = Sems()

    nsrc = (nz, ny)
    nq = (ny * nc, nz * nc)
    me_src = (z, y)
    me_q = (yc, zc)

    def src_dev(kind, p):
        return (p * ny + y) * nc + c if kind == 0 else (z * ny + p) * nc + c

    def q_dev(kind, q):
        return z * ny * nc + q if kind == 0 else ((q // nc) * ny + y) * nc + q % nc

    half = (nq[0] * nsrc[0] * 2, nq[1] * nsrc[1] * 2)
    base = (0, half[0])
    total = half[0] + half[1]
    blk = total // xs
    ntok = (nsrc[0] * tok, nsrc[1] * tok)

    def rdma(src, dst, sem, dev):
        return pltpu.make_async_remote_copy(
            src_ref=src, dst_ref=dst, send_sem=ssem.at[sem], recv_sem=rsem.at[sem],
            device_id=dev, device_id_type=MESH,
        )

    started = []

    def wait_recv(ref, sem):
        rdma(ref, ref, sem, (i, e)).wait_recv()

    def note_send(ref, sem):
        started.append((ref, sem))

    loads = [
        pltpu.make_async_copy(wg_hbm.at[0], wgu.at[:, pl.ds(0, ff)], wsem.at[0]),
        pltpu.make_async_copy(wu_hbm.at[0], wgu.at[:, pl.ds(ff, ff)], wsem.at[1]),
        pltpu.make_async_copy(wd_hbm.at[0], wd, wsem.at[2]),
    ]
    for load in loads:
        load.start()

    barrier = pltpu.get_barrier_semaphore()
    for k in range(1, xs):
        pl.semaphore_signal(barrier, inc=1, device_id=((i + k) % xs, e), device_id_type=MESH)
    for kind in range(2):
        @pl.loop(1, nq[kind])
        def _(k, kind=kind):
            peer = q_dev(kind, (me_q[kind] + k) % nq[kind])
            pl.semaphore_signal(barrier, inc=1, device_id=(i, peer), device_id_type=MESH)
    pl.semaphore_wait(barrier, xs - 1 + nq[0] - 1 + nq[1] - 1)

    info_refs = (routes_ref, gates_ref)
    data_refs = (tok_ref, cot_ref)
    x_sems = []
    for t in range(2):
        si, sd = sems.take(1), sems.take(1)
        x_sems.append((si, sd))
        for k in range(1, xs):
            peer = (i + k) % xs
            rdma(info_refs[t], xinfo.at[t, i], si, (peer, e)).start()
            rdma(
                data_refs[t].at[:, pl.ds(pl.multiple_of(peer * dq, 128), dq)],
                xdata.at[t, i], sd, (peer, e),
            ).start()
        xinfo[t, i] = info_refs[t][...]
        xdata[t, i] = data_refs[t][:, pl.ds(pl.multiple_of(i * dq, 128), dq)]
        note_send(xinfo.at[t, pl.ds(0, xs - 1)], si)
        note_send(xdata.at[t, pl.ds(0, xs - 1)], sd)

    g_sems = [[None] * 2 for _ in range(2)]
    d_sems = [[[None] * 2 for _ in range(2)] for _ in range(2)]
    for t in range(2):
        si, sd = x_sems[t]
        wait_recv(xinfo.at[t, pl.ds(0, xs - 1)], si)
        wait_recv(xdata.at[t, pl.ds(0, xs - 1)], sd)
        for kind in range(2):
            g_sems[t][kind] = sems.take(1)
            n = nsrc[kind]

            @pl.loop(1, n)
            def _(k, t=t, kind=kind, n=n):
                p = (me_src[kind] + k) % n
                rdma(
                    xinfo.at[t, pl.ds(2 * kind, 2)], ginfo.at[t, kind, me_src[kind]],
                    g_sems[t][kind], (i, src_dev(kind, p)),
                ).start()
            ginfo[t, kind, me_src[kind]] = xinfo[t, 2 * kind : 2 * kind + 2]
            note_send(ginfo.at[t, kind, pl.ds(0, n - 1)], g_sems[t][kind])
        for s in range(2):
            for kind in range(2):
                d_sems[t][s][kind] = sem = sems.take(1)
                n = nsrc[kind]

                @pl.loop(1, n)
                def _(k, t=t, s=s, kind=kind, n=n, sem=sem):
                    p = (me_src[kind] + k) % n
                    rdma(
                        xdata.at[t, 2 * kind + s],
                        gdata.at[t, s, kind, pl.ds(pl.multiple_of(me_src[kind] * tok, tok), tok)],
                        sem, (i, src_dev(kind, p)),
                    ).start()
                gdata[t, s, kind, pl.ds(pl.multiple_of(me_src[kind] * tok, tok), tok)] = xdata[
                    t, 2 * kind + s
                ]
                note_send(gdata.at[t, s, kind, pl.ds(0, (n - 1) * tok)], sem)

    def q_exchange(src, dst, kind):
        sem = sems.take(1)
        n, size = nq[kind], nsrc[kind] * 2
        mine = pl.ds(pl.multiple_of(base[kind] + me_q[kind] * size, size), size)

        @pl.loop(1, n)
        def _(k):
            q = (me_q[kind] + k) % n
            rdma(
                src.at[pl.ds(pl.multiple_of(base[kind] + q * size, size), size)],
                dst.at[mine], sem, (i, q_dev(kind, q)),
            ).start()
        dst[mine] = src[mine]
        view = dst.at[pl.ds(base[kind], (n - 1) * size)]
        note_send(view, sem)
        return view, sem

    lane = lax.broadcasted_iota(jnp.int32, (1, 128), 1) // tok

    def gathered(t, s, kind):
        tile = jnp.zeros((8, 128), F32)
        for p in range(nsrc[kind]):
            tile = jnp.where(lane == p, ginfo[t, kind, p, s], tile)
        return tile

    def matches(kind, s):
        tile = gathered(0, s, kind)
        q = lax.broadcasted_iota(jnp.int32, (nq[kind], 128), 0)
        wanted = q_dev(kind, q).astype(F32)
        return [tile[k : k + 1] == wanted for k in range(8)]

    seg_r = lax.broadcasted_iota(jnp.int32, (128, 128), 0)
    seg_c = lax.broadcasted_iota(jnp.int32, (128, 128), 1)
    earlier = jnp.where((seg_r // tok == seg_c // tok) & (seg_r < seg_c), 1.0, 0.0).astype(BF16)

    for t in range(1):
        for kind in range(2):
            wait_recv(ginfo.at[t, kind, pl.ds(0, nsrc[kind] - 1)], g_sems[t][kind])
    for s in range(2):
        for kind in range(2):
            hit = jnp.zeros((nq[kind], 128), F32)
            for m in matches(kind, s):
                hit = jnp.where(m, 1.0, hit)
            prior = jnp.dot(hit.astype(BF16), earlier, preferred_element_type=F32)
            first = jnp.where(prior < 0.5, hit, 0.0)
            second = hit - first
            size = nsrc[kind] * 2
            r = lax.broadcasted_iota(jnp.int32, (size, 128), 0)
            cell = lax.broadcasted_iota(jnp.int32, (size, 128), 1) // tok == r // 2
            seg0 = jnp.where(cell & (r % 2 == 0), 1.0, 0.0)
            seg1 = jnp.where(cell & (r % 2 == 1), 1.0, 0.0)
            for q in range(nq[kind]):
                dmat[s, pl.ds(base[kind] + q * size, size), :] = (
                    seg0 * first[q : q + 1] + seg1 * second[q : q + 1]
                ).astype(BF16)

    arrivals = [[[None] * 2 for _ in range(2)] for _ in range(2)]

    def send_rows(t, s):
        for kind in range(2):
            wait_recv(gdata.at[t, s, kind, pl.ds(0, (nsrc[kind] - 1) * tok)], d_sems[t][s][kind])
            span = pl.ds(base[kind], half[kind])
            picked = jnp.dot(
                dmat[s, span, : ntok[kind]], gdata[t, s, kind, : ntok[kind]],
                preferred_element_type=F32,
            )
            if t == 1:
                picked = picked * gcol[s, span, :]
            rows[t, s, span, :] = picked.astype(BF16)
            arrivals[t][s][kind] = q_exchange(rows.at[t, s], recv.at[t, s], kind)

    for s in range(2):
        send_rows(0, s)

    for kind in range(2):
        wait_recv(ginfo.at[1, kind, pl.ds(0, nsrc[kind] - 1)], g_sems[1][kind])
    for s in range(2):
        for kind in range(2):
            tile = gathered(1, s, kind)
            gate = jnp.zeros((nq[kind], 128), F32)
            for k, m in enumerate(matches(kind, s)):
                gate = jnp.where(m, tile[k : k + 1], gate)
            size = nsrc[kind] * 2
            for q in range(nq[kind]):
                span = pl.ds(base[kind] + q * size, size)
                w = dmat[s, span, :].astype(F32) * gate[q : q + 1]
                hi = w.astype(BF16)
                whi[s, span, :] = hi
                wlo[s, span, :] = (w - hi.astype(F32)).astype(BF16)
                gcol[s, span, :] = jnp.sum(w, axis=1, keepdims=True)

    for s in range(2):
        send_rows(1, s)

    def chunk(k):
        return pl.ds(pl.multiple_of(k * blk, blk), blk)

    def ring_sum_1(p, r, w):
        sem = sems.take(6)
        a, b = pl.ds(0, w), pl.ds(w, w)
        sends = (
            (p.at[chunk(opp), a], 0, right), (p.at[chunk(opp), b], 1, left),
            (p.at[chunk(left), a], 2, left), (p.at[chunk(right), b], 3, right),
        )
        for src, slot, dev in sends:
            rdma(src, r.at[slot], sem + slot, (dev, e)).start()
            note_send(r.at[slot], sem + slot)
        return sem

    def ring_sum_2(p, r, w, sem):
        for slot, lanes, dev in ((0, pl.ds(0, w), right), (1, pl.ds(w, w), left)):
            wait_recv(r.at[slot], sem + slot)
            r[6 + slot] = (
                r[slot].astype(F32) + p[chunk(dev), lanes].astype(F32)
            ).astype(BF16)
            rdma(r.at[6 + slot], r.at[4 + slot], sem + 4 + slot, (dev, e)).start()
            note_send(r.at[4 + slot], sem + 4 + slot)

    def ring_sum_3(p, r, w, sem):
        for slot in range(2, 6):
            wait_recv(r.at[slot], sem + slot)
        a = p[chunk(i), :w].astype(F32) + r[2].astype(F32) + r[4].astype(F32)
        b = p[chunk(i), w:].astype(F32) + r[3].astype(F32) + r[5].astype(F32)
        return a, b

    def ring_gather_1(g):
        sem = sems.take(4)
        rdma(g.at[chunk(i)], g.at[chunk(i)], sem, (right, e)).start()
        rdma(g.at[chunk(i)], g.at[chunk(i)], sem + 1, (left, e)).start()
        note_send(g.at[chunk(i)], sem)
        note_send(g.at[chunk(i)], sem + 1)
        return sem

    def ring_gather_2(g, w, sem):
        for k, frm, dev in ((0, left, right), (1, right, left)):
            wait_recv(g.at[chunk(frm)], sem + k)
            view = g.at[chunk(frm), pl.ds(k * w, w)]
            rdma(view, view, sem + 2 + k, (dev, e)).start()
            note_send(view, sem + 2 + k)

    def ring_gather_3(g, w, sem):
        for k in range(2):
            wait_recv(g.at[chunk(opp), pl.ds(k * w, w)], sem + 2 + k)

    CONTRACT_LAST = (((1,), (1,)), ((), ()))
    CONTRACT_FIRST = (((0,), (0,)), ((), ()))

    def rows_ready(t, s):
        for kind in range(2):
            view, sem = arrivals[t][s][kind]
            wait_recv(view, sem)

    tn = fit(2 * ff, 256)
    tf = fit(ff, 256)
    td = fit(dq, 256)

    def gate_up(s):
        rows_ready(0, s)

        @pl.loop(0, 2 * ff // tn)
        def _(n):
            cols = pl.ds(pl.multiple_of(n * tn, tn), tn)
            pgu[s, :, cols] = jnp.dot(
                recv[0, s], wgu[:, cols], preferred_element_type=F32
            ).astype(BF16)
        return ring_sum_1(pgu.at[s], rgu.at[s], ff)

    def d_hidden(s):
        rows_ready(1, s)

        @pl.loop(0, ff // tf)
        def _(n):
            cols = pl.ds(pl.multiple_of(n * tf, tf), tf)
            pdh[s, :, cols] = lax.dot_general(
                recv[1, s], wd[cols, :], CONTRACT_LAST, preferred_element_type=F32
            ).astype(BF16)
        return ring_sum_1(pdh.at[s], rdh.at[s], ff // 2)

    def hidden(s, sem):
        gate, up = ring_sum_3(pgu.at[s], rgu.at[s], ff, sem)
        gate_s[s, 0] = gate
        gate_s[s, 1] = up
        hid[s, chunk(i), :] = (gate * jax.nn.sigmoid(gate) * up).astype(BF16)
        return ring_gather_1(hid.at[s])

    def d_gate_up(s, sem):
        w = ff // 2
        parts = ring_sum_3(pdh.at[s], rdh.at[s], w, sem)
        for k in range(2):
            cols = slice(k * w, (k + 1) * w)
            gate, up, dh = gate_s[s, 0, :, cols], gate_s[s, 1, :, cols], parts[k]
            sig = jax.nn.sigmoid(gate)
            dgu[s, chunk(i), pl.ds(k * w, w)] = (
                dh * up * sig * (1.0 + gate * (1.0 - sig))
            ).astype(BF16)
            dgu[s, chunk(i), pl.ds(ff + k * w, w)] = (dh * (gate * sig)).astype(BF16)
        return ring_gather_1(dgu.at[s])

    def out_rows(s):
        @pl.loop(0, dq // td)
        def _(n):
            cols = pl.ds(pl.multiple_of(n * td, td), td)
            ret_s[0, s, :, cols] = jnp.dot(
                hid[s], wd[:, cols], preferred_element_type=F32
            ).astype(BF16)
        return [q_exchange(ret_s.at[0, s], ret.at[0, s], kind) for kind in range(2)]

    def back_rows(s):
        @pl.loop(0, dq // td)
        def _(n):
            cols = pl.ds(pl.multiple_of(n * td, td), td)
            ret_s[1, s, :, cols] = lax.dot_general(
                dgu[s], wgu[cols, :], CONTRACT_LAST, preferred_element_type=F32
            ).astype(BF16)
        return [q_exchange(ret_s.at[1, s], ret.at[1, s], kind) for kind in range(2)]

    def combine(t, s, arrived):
        result = []
        for kind in range(2):
            wait_recv(*arrived[kind])
            span = pl.ds(base[kind], half[kind])
            got = ret[t, s, span, :]
            if t == 0:
                sums = lax.dot_general(
                    whi[s, span, :], got, CONTRACT_FIRST, preferred_element_type=F32
                ) + lax.dot_general(
                    wlo[s, span, :], got, CONTRACT_FIRST, preferred_element_type=F32
                )
            else:
                sums = lax.dot_general(
                    dmat[s, span, :], got, CONTRACT_FIRST, preferred_element_type=F32
                )
            part[t, s, kind] = sums[: ntok[kind]].astype(BF16)
            sem = sems.take(1)
            n = nsrc[kind]
            mine = pl.ds(pl.multiple_of(me_src[kind] * tok, tok), tok)

            @pl.loop(1, n)
            def _(k, kind=kind, n=n, sem=sem, mine=mine):
                p = (me_src[kind] + k) % n
                rdma(
                    part.at[t, s, kind, pl.ds(pl.multiple_of(p * tok, tok), tok)],
                    psum.at[t, s, kind, mine], sem, (i, src_dev(kind, p)),
                ).start()
            psum[t, s, kind, mine] = part[t, s, kind, mine]
            view = psum.at[t, s, kind, pl.ds(0, (n - 1) * tok)]
            note_send(view, sem)
            result.append((view, sem))
        return result

    def finish(t, s, arrived):
        for kind in range(2):
            wait_recv(*arrived[kind])
            acc = psum[t, s, kind, :tok].astype(F32)
            for p in range(1, nsrc[kind]):
                acc = acc + psum[t, s, kind, p * tok : (p + 1) * tok].astype(F32)
            fin[t, 2 * kind + s] = acc.astype(BF16)

    def give_back(t):
        sem = sems.take(1)
        lanes = pl.ds(pl.multiple_of(i * dq, 128), dq)
        for k in range(1, xs):
            peer = (i + k) % xs
            rdma(fin.at[t, peer], land.at[t, i], sem, (peer, e)).start()
        land[t, i] = fin[t, i]
        view = land.at[t, pl.ds(0, xs - 1)]
        note_send(view, sem)
        return view, sem

    def grad_down(s):
        @pl.loop(0, ff // tf)
        def _(n):
            cols = pl.ds(pl.multiple_of(n * tf, tf), tf)
            value = lax.dot_general(
                hid[s, :, cols], recv[1, s], CONTRACT_FIRST, preferred_element_type=F32
            )
            if s == 0:
                gdacc[cols, :] = value
            else:
                gd_ref[0, cols, :] = (gdacc[cols, :] + value).astype(BF16)

    def grad_gate_up(s):
        for k, ref in ((0, gg_ref), (1, gu_ref)):
            @pl.loop(0, ff // tf)
            def _(n, k=k, ref=ref):
                cols = pl.ds(pl.multiple_of(n * tf, tf), tf)
                both = pl.ds(pl.multiple_of(k * ff + n * tf, tf), tf)
                value = lax.dot_general(
                    recv[0, s], dgu[s, :, both], CONTRACT_FIRST, preferred_element_type=F32
                )
                if s == 0:
                    gacc[:, both] = value
                else:
                    ref[0, :, cols] = (gacc[:, both] + value).astype(BF16)

    loads[0].wait()
    loads[1].wait()
    gu0 = gate_up(0)
    gu1 = gate_up(1)
    ring_sum_2(pgu.at[0], rgu.at[0], ff, gu0)
    loads[2].wait()
    dh0 = d_hidden(0)
    ring_sum_2(pgu.at[1], rgu.at[1], ff, gu1)
    dh1 = d_hidden(1)
    h0 = hidden(0, gu0)
    ring_sum_2(pdh.at[0], rdh.at[0], ff // 2, dh0)
    h1 = hidden(1, gu1)
    ring_sum_2(pdh.at[1], rdh.at[1], ff // 2, dh1)
    g0 = d_gate_up(0, dh0)
    ring_gather_2(hid.at[0], ff // 2, h0)
    g1 = d_gate_up(1, dh1)
    ring_gather_2(hid.at[1], ff // 2, h1)
    ring_gather_3(hid.at[0], ff // 2, h0)
    o0 = out_rows(0)
    grad_down(0)
    ring_gather_2(dgu.at[0], ff, g0)
    ring_gather_3(hid.at[1], ff // 2, h1)
    o1 = out_rows(1)
    ring_gather_2(dgu.at[1], ff, g1)
    co0 = combine(0, 0, o0)
    grad_down(1)
    ring_gather_3(dgu.at[0], ff, g0)
    b0 = back_rows(0)
    co1 = combine(0, 1, o1)
    grad_gate_up(0)
    ring_gather_3(dgu.at[1], ff, g1)
    b1 = back_rows(1)
    finish(0, 0, co0)
    finish(0, 1, co1)
    land_o = give_back(0)
    cb0 = combine(1, 0, b0)
    grad_gate_up(1)
    cb1 = combine(1, 1, b1)
    wait_recv(*land_o)
    for j in range(xs):
        out_ref[:, j * dq : (j + 1) * dq] = land[0, j]
    finish(1, 0, cb0)
    finish(1, 1, cb1)
    land_b = give_back(1)
    wait_recv(*land_b)
    for j in range(xs):
        dtok_ref[:, j * dq : (j + 1) * dq] = land[1, j]
    for ref, sem in started:
        rdma(ref, ref, sem, (i, e)).wait_send()
    assert sems.count <= ssem.shape[0]


def local(shape, tokens, routes, gates, cotangent, w_gate, w_up, w_down):
    nz, ny, nc = shape
    tok, features = tokens.shape
    fanout = routes.shape[1]
    xs = 4
    dq, ff = w_gate.shape[1], w_gate.shape[2]
    copies = 128 // tok
    spread = lambda v: jnp.tile(v.astype(F32).T, (1, copies))
    half = (ny * nc * nz * 2, nz * nc * ny * 2)
    total = half[0] + half[1]
    blk = total // xs
    most = max(nz, ny)
    gtok = most * tok
    V = pltpu.VMEM
    nsem = 96
    vm = pl.BlockSpec(memory_space=pltpu.VMEM)
    hb = pl.BlockSpec(memory_space=pl.ANY)
    sds = jax.ShapeDtypeStruct
    return pl.pallas_call(
        functools.partial(body, (nz, ny, nc, dq, ff, tok)),
        out_shape=(
            sds((tok, features), BF16), sds((tok, features), BF16),
            sds(w_gate.shape, BF16), sds(w_up.shape, BF16), sds(w_down.shape, BF16),
        ),
        in_specs=[vm, vm, vm, vm, hb, hb, hb],
        out_specs=(vm, vm, vm, vm, vm),
        scratch_shapes=[
            V((dq, 2 * ff), BF16),
            V((ff, dq), BF16),
            V((2, xs, fanout, 128), F32),
            V((2, xs, tok, dq), BF16),
            V((2, 2, most, 2, fanout, 128), F32),
            V((2, 2, 2, gtok, dq), BF16),
            V((2, total, 128), BF16),
            V((2, total, 128), BF16),
            V((2, total, 128), BF16),
            V((2, total, 1), F32),
            V((2, 2, total, dq), BF16),
            V((2, 2, total, dq), BF16),
            V((2, total, 2 * ff), BF16),
            V((2, total, ff), BF16),
            V((2, 8, blk, ff), BF16),
            V((2, 8, blk, ff // 2), BF16),
            V((2, total, ff), BF16),
            V((2, total, 2 * ff), BF16),
            V((2, 2, blk, ff), F32),
            V((dq, 2 * ff), F32),
            V((ff, dq), F32),
            V((2, 2, total, dq), BF16),
            V((2, 2, total, dq), BF16),
            V((2, 2, 2, gtok, dq), BF16),
            V((2, 2, 2, gtok, dq), BF16),
            V((2, xs, tok, dq), BF16),
            V((2, xs, tok, dq), BF16),
            pltpu.SemaphoreType.DMA((3,)),
            pltpu.SemaphoreType.DMA((nsem,)),
            pltpu.SemaphoreType.DMA((nsem,)),
        ],
        compiler_params=pltpu.CompilerParams(
            collective_id=0, has_side_effects=True, vmem_limit_bytes=60 * 1024 * 1024
        ),
        name="moe_layer",
    )(spread(routes), spread(gates), tokens, cotangent, w_gate, w_up, w_down)


def solution(mesh):
    return jax.shard_map(
        functools.partial(local, LAYOUT[mesh.shape["expert"]]),
        mesh=mesh,
        in_specs=(
            P(("dp", "expert"), None),
            P(("dp", "expert"), None),
            P(("dp", "expert"), None),
            P(("dp", "expert"), None),
            P("expert", "dp", None),
            P("expert", "dp", None),
            P("expert", None, "dp"),
        ),
        out_specs=(
            P(("dp", "expert"), None),
            P(("dp", "expert"), None),
            P("expert", "dp", None),
            P("expert", "dp", None),
            P("expert", None, "dp"),
        ),
        check_vma=False,
    )
```

time: 424 us -> 166 us (0.39)
  waiting for transfers between devices: 214 us -> 0 us
  Pallas kernels: 0 us -> 156 us
  blocking collectives: 78.3 us -> 0 us
  starting transfers between devices: 40.5 us -> 0 us
  matrix products: 31.2 us -> 0 us
  local copies, waits for them, and re-layouts: 34.2 us -> 7.94 us
  between operations: 14 us -> 0.66 us
  other arithmetic: 10.5 us -> 0.69 us
    pallas_call x0 -> x1, Pallas kernels: none -> 156 us  [local(): pl.pallas_call(functools.partial(body, (nz, ny, nc, dq, ff, tok)), out_sh...]
    all_to_all x6 -> x0, waiting for transfers between devices: 87.3 us -> none  [the longest x1 26.2 us: local(): lax.all_to_all(returned[0], 'expert', split_axis=1, concat_axis=1, tiled=...]
    all_to_all x2 -> x0, blocking collectives: 78.3 us -> none  [the longest x1 49.2 us: local(): lax.all_to_all(send_input, 'expert', split_axis=1, concat_axis=1, tiled=T...]
    all_gather x2 -> x0, waiting for transfers between devices: 58.2 us -> none  [the longest x1 30 us: local(): lax.all_gather(dup_own, 'dp', axis=0, tiled=True)]
    psum x1 -> x0, waiting for transfers between devices: 40.5 us -> none  [local(): lax.psum(up_part.astype(jnp.bfloat16), 'dp').astype(jnp.float32)]
    all_to_all x6 -> x0, starting transfers between devices: 40.1 us -> none  [the longest x1 15.3 us: local(): lax.all_to_all(returned[0], 'expert', split_axis=1, concat_axis=1, tiled=...]
    dot_general x16 -> x0, matrix products: 31.2 us -> none  [the longest x1 4.39 us: local(): jnp.einsum('rf,df->rd', dup_all, up_local, preferred_element_type=jnp.flo...]
    reduce_scatter x1 -> x0, waiting for transfers between devices: 27.7 us -> none  [local(): lax.psum_scatter(dhidden_part.astype(jnp.bfloat16), 'dp', scatter_dimensi...]
  transfers between devices with their start and end apart: 10 -> 0, of which waited for: 9 -> 0; matrix products, arithmetic and copies ran while one was open for 15% -> 0% of each run, Pallas kernels for 0% -> 0%
where the time goes in v1:
time: 166 us
  Pallas kernels  156 us (94%)
  local copies, waits for them, and re-layouts  7.94 us (5%)
    pallas_call x1, Pallas kernels, local(): pl.pallas_call(functools.partial(body, (nz, ny, nc, dq, ff, tok)), out_sh...  156 us
    unnamed x13, local copies, waits for them, and re-layouts  6.59 us

profile of v1, /device:TPU:1, one launch (start us, length us, event | category | flops | bytes accessed | tf_op | source)
XLA Modules:
  0.0 165.5 jit_solution(6204370570741877336)
XLA Ops:
  0.6 0.7 convert_bitcast_fusion
  1.3 0.0 copy-start.3
  1.3 0.7 tile.9.routes_ref
  2.0 0.0 copy-done.3
  2.0 0.7 tile.21.gates_ref
  2.7 156.3 %moe_layer.1 = (bf16[16,2048]{1,0:T(8,128)(2,1)}, bf16[16,2048]{1,0:T(8,128)(2,1)}, bf16[1,512,768]{2,1,0:T(8,128)(2,1)}, bf16[1,512,768]{2,1,0:T(8,128)(2,1)}, bf16[1,768,512]{2,1,0:T(8,128)(2,1)}) custom-call(f32[8,128]{1,0:T(8,128)} %tile.9.routes_ref, f32[8,128]{1,0:T(8,128)} %tile.21.gates_ref, bf16[16,2048]{1,0:T(8,128)(2,1)} %tok_ref.1, ...), custom_call_target="tpu_custom_call" | custom-call | tf_op jit(solution)/shard_map/moe_layer/pallas_call | solution.py:517
  159.0 0.0 copy-start.2
  159.0 1.5 copy.17
  160.5 0.0 copy-done.2
  160.5 0.6 copy.18
  161.1 0.0 copy-start.1
  161.1 2.1 %copy.19 = bf16[1,512,768]{2,1,0:T(8,128)(2,1)} copy(bf16[1,512,768]{2,1,0:T(8,128)(2,1)} %get-tuple-element.12) | data formatting | bytes 1572864
  163.2 0.0 copy-done.1
  163.2 0.0 copy-start
  163.2 0.9 copy.20
  164.1 0.5 copy-done
  164.7 0.9 copy.21
  (2 shorter events, 0.0 us)
Async XLA Ops:
  1.3 0.7 copy-start.3
  159.0 1.5 copy-start.2
  161.1 2.1 %copy-start.1 = (bf16[1,512,768]{2,1,0:T(8,128)(2,1)S(1)}, bf16[1,512,768]{2,1,0:T(8,128)(2,1)}, u32[]{:S(2)}) copy-start(bf16[1,512,768]{2,1,0:T(8,128)(2,1)} %get-tuple-element.13) | copy-start | bytes 2359300
  163.2 1.4 copy-start

commit v2 on v1

v2 whole, which is shorter than its diff:
```python
import functools

import jax
import jax.numpy as jnp
from jax import lax
from jax.experimental import pallas as pl
from jax.experimental.pallas import tpu as pltpu
from jax.sharding import PartitionSpec as P

MESH = pl.DeviceIdType.MESH
LAYOUT = {128: (8, 8, 2), 8: (2, 2, 2)}
F32, BF16 = jnp.float32, jnp.bfloat16
CONTRACT_LAST = (((1,), (1,)), ((), ()))
CONTRACT_FIRST = (((0,), (0,)), ((), ()))


def fit(total, want):
    return want if total % want == 0 else total


class Sems:
    def __init__(self):
        self.count = 0

    def take(self, n):
        first = self.count
        self.count += n
        return first


def body(
    cfg,
    routes_ref, gates_ref, tok_ref, cot_ref, wg_hbm, wu_hbm, wd_hbm,
    out_hbm, dtok_hbm, gg_hbm, gu_hbm, gd_hbm,
    raw_r, raw_g, own_r, own_g, wgu, wd, xroutes, xgates, xdata, groutes, ggates, gdata, dmat, whi, wlo, gcol,
    rows, recv, pgu, pdh, rgu, rdh, hid, dgu, gate_s, gacc, gdacc,
    ret_s, ret, part, psum, fin, land, gg, gu, gd, tok_out,
    wsem, osem, ssem, rsem,
):
    n8, nc, dq, ff, tok = cfg
    xs = 4
    nq = n8 * nc
    qc = nq // xs
    size = 2 * n8
    blk = 2 * qc * size
    gt = n8 * tok
    i = lax.axis_index("dp")
    e = lax.axis_index("expert")
    z, yc = e // nq, e % nq
    y, c = yc // nc, yc % nc
    right, left, opp = (i + 1) % xs, (i + 3) % xs, (i + 2) % xs
    sems = Sems()

    me_src = (z, y)
    me_q = (yc, z * nc + c)

    def src_dev(kind, p):
        return (p * n8 + y) * nc + c if kind == 0 else (z * n8 + p) * nc + c

    def q_dev(kind, q):
        return z * nq + q if kind == 0 else ((q // nc) * n8 + y) * nc + q % nc

    def q_rows(kind, q):
        at = (q // qc) * blk + kind * (qc * size) + (q % qc) * size
        return pl.ds(at if isinstance(at, int) else pl.multiple_of(at, size), size)

    def src_rows(kind, p):
        return pl.ds(pl.multiple_of(kind * gt + p * tok, tok), tok)

    def rdma(src, dst, sem, dev):
        return pltpu.make_async_remote_copy(
            src_ref=src, dst_ref=dst, send_sem=ssem.at[sem], recv_sem=rsem.at[sem],
            device_id=dev, device_id_type=MESH,
        )

    started = []

    def wait_recv(ref, sem):
        rdma(ref, ref, sem, (i, e)).wait_recv()

    def note_send(ref, sem):
        started.append((ref, sem))

    part_of = lambda ref, k: ref.at[:, pl.ds(pl.multiple_of(k * dq, 128), dq)]
    owns = [
        pltpu.make_async_copy(routes_ref, raw_r, wsem.at[3]),
        pltpu.make_async_copy(part_of(tok_ref, i), xdata.at[0, i], wsem.at[4]),
        pltpu.make_async_copy(gates_ref, raw_g, wsem.at[5]),
        pltpu.make_async_copy(part_of(cot_ref, i), xdata.at[1, i], wsem.at[6]),
    ]
    for own in owns:
        own.start()
    loads = [
        pltpu.make_async_copy(wg_hbm.at[0], wgu.at[:, pl.ds(0, ff)], wsem.at[0]),
        pltpu.make_async_copy(wu_hbm.at[0], wgu.at[:, pl.ds(ff, ff)], wsem.at[1]),
        pltpu.make_async_copy(wd_hbm.at[0], wd, wsem.at[2]),
    ]
    for load in loads:
        load.start()
    for t, raw, tile_ref in ((0, raw_r, own_r), (1, raw_g, own_g)):
        owns[2 * t].wait()
        value = raw[...]
        blank = jnp.zeros((value.shape[0], 128 - tok), value.dtype)
        tile_ref[...] = jnp.concatenate([value, blank], axis=1)

    with jax.named_scope("h_barrier"):
        barrier = pltpu.get_barrier_semaphore()
        for k in range(1, xs):
            pl.semaphore_signal(barrier, inc=1, device_id=((i + k) % xs, e), device_id_type=MESH)
        for kind in range(2):
            @pl.loop(1, nq)
            def _(k, kind=kind):
                peer = q_dev(kind, (me_q[kind] + k) % nq)
                pl.semaphore_signal(barrier, inc=1, device_id=(i, peer), device_id_type=MESH)
        pl.semaphore_wait(barrier, xs - 1 + 2 * (nq - 1))

    info = ((own_r, xroutes, groutes), (own_g, xgates, ggates))
    data_refs = (tok_ref, cot_ref)
    x_sems = []
    with jax.named_scope("h_x"):
        for t in range(2):
            own, xinfo, _ = info[t]
            si, sd = sems.take(1), sems.take(1)
            x_sems.append((si, sd))
            for k in (2, 1, 3):
                peer = (i + k) % xs
                rdma(own, xinfo.at[i], si, (peer, e)).start()
                rdma(part_of(data_refs[t], peer), xdata.at[t, i], sd, (peer, e)).start()
            xinfo[i] = own[...]
            note_send(xinfo.at[pl.ds(0, xs - 1)], si)
            note_send(xdata.at[t, pl.ds(0, xs - 1)], sd)

    def gather_info(t):
        _, xinfo, ginfo = info[t]
        wait_recv(xinfo.at[pl.ds(0, xs - 1)], x_sems[t][0])
        sem = sems.take(1)
        for kind in range(2):
            @pl.loop(1, n8)
            def _(k, kind=kind, sem=sem):
                rdma(
                    xinfo.at[pl.ds(2 * kind, 2)], ginfo.at[kind, me_src[kind]],
                    sem, (i, src_dev(kind, (me_src[kind] + k) % n8)),
                ).start()
            ginfo[kind, me_src[kind]] = xinfo[2 * kind : 2 * kind + 2]
        view = ginfo.at[:, pl.ds(0, n8 - 1)]
        note_send(view, sem)
        return [(view, sem)]

    def gather_data(t, s):
        sem = sems.take(1)
        for kind in range(2):
            @pl.loop(1, n8)
            def _(k, kind=kind, sem=sem):
                rdma(
                    xdata.at[t, 2 * kind + s], gdata.at[t, s, src_rows(kind, me_src[kind])],
                    sem, (i, src_dev(kind, (me_src[kind] + k) % n8)),
                ).start()
            gdata[t, s, src_rows(kind, me_src[kind])] = xdata[t, 2 * kind + s]
        view = gdata.at[t, s, pl.ds(0, 2 * (n8 - 1) * tok)]
        note_send(view, sem)
        return [(view, sem)]

    def wait_all(pairs):
        for view, sem in pairs:
            wait_recv(view, sem)

    def exchange(src, dst):
        sem = sems.take(1)
        for kind in range(2):
            mine = q_rows(kind, me_q[kind])

            @pl.loop(1, nq)
            def _(k, kind=kind, sem=sem, mine=mine):
                q = (me_q[kind] + k) % nq
                rdma(src.at[q_rows(kind, q)], dst.at[mine], sem, (i, q_dev(kind, q))).start()
            dst[mine] = src[mine]
        view = dst.at[pl.ds(0, 2 * (nq - 1) * size)]
        note_send(view, sem)
        return [(view, sem)]

    def tile(ginfo, s, kind):
        return jnp.concatenate([ginfo[kind, p, s][:, :tok] for p in range(n8)], axis=1)

    def matches(s, kind):
        names = tile(groutes, s, kind)
        wanted = q_dev(kind, lax.broadcasted_iota(jnp.int32, (nq, gt), 0))
        return [names[k : k + 1] == wanted for k in range(names.shape[0])]

    before_r = lax.broadcasted_iota(jnp.int32, (gt, gt), 0)
    before_c = lax.broadcasted_iota(jnp.int32, (gt, gt), 1)
    earlier = jnp.where(
        (before_r // tok == before_c // tok) & (before_r < before_c), 1.0, 0.0
    ).astype(BF16)
    slot_r = lax.broadcasted_iota(jnp.int32, (size, gt), 0)
    cell = lax.broadcasted_iota(jnp.int32, (size, gt), 1) // tok == slot_r // 2
    seg0 = jnp.where(cell & (slot_r % 2 == 0), 1.0, 0.0)
    seg1 = jnp.where(cell & (slot_r % 2 == 1), 1.0, 0.0)

    def selection(s):
        nothing = jnp.zeros((size, gt), BF16)
        for kind in range(2):
            hit = jnp.zeros((nq, gt), F32)
            for m in matches(s, kind):
                hit = jnp.where(m, 1.0, hit)
            prior = jnp.dot(hit.astype(BF16), earlier, preferred_element_type=F32)
            first = jnp.where(prior < 0.5, hit, 0.0)
            second = hit - first
            for q in range(nq):
                dmat[s, q_rows(kind, q), pl.ds(kind * gt, gt)] = (
                    seg0 * first[q : q + 1] + seg1 * second[q : q + 1]
                ).astype(BF16)
                dmat[s, q_rows(kind, q), pl.ds((1 - kind) * gt, gt)] = nothing

    def weighting(s):
        nothing = jnp.zeros((size, gt), BF16)
        for kind in range(2):
            values = tile(ggates, s, kind)
            gate = jnp.zeros((nq, gt), F32)
            for k, m in enumerate(matches(s, kind)):
                gate = jnp.where(m, values[k : k + 1], gate)
            for q in range(nq):
                w = dmat[s, q_rows(kind, q), pl.ds(kind * gt, gt)].astype(F32) * gate[q : q + 1]
                hi = w.astype(BF16)
                whi[s, q_rows(kind, q), pl.ds(kind * gt, gt)] = hi
                wlo[s, q_rows(kind, q), pl.ds(kind * gt, gt)] = (w - hi.astype(F32)).astype(BF16)
                whi[s, q_rows(kind, q), pl.ds((1 - kind) * gt, gt)] = nothing
                wlo[s, q_rows(kind, q), pl.ds((1 - kind) * gt, gt)] = nothing
                gcol[s, q_rows(kind, q), :] = jnp.sum(w, axis=1, keepdims=True)

    def send_rows(t, s, gathered):
        wait_all(gathered)
        picked = jnp.dot(dmat[s], gdata[t, s], preferred_element_type=F32)
        if t == 1:
            picked = picked * gcol[s]
        rows[t, s] = picked.astype(BF16)
        return exchange(rows.at[t, s], recv.at[t, s])

    def chunk(k):
        return pl.ds(pl.multiple_of(k * blk, blk), blk)

    def ring_part(p, r, w, sem, which):
        a, b = pl.ds(0, w), pl.ds(w, w)
        for slot in which:
            at, lanes, dev = (
                (opp, a, right), (opp, b, left), (left, a, left), (right, b, right)
            )[slot]
            rdma(p.at[chunk(at), lanes], r.at[slot], sem + slot, (dev, e)).start()
            note_send(r.at[slot], sem + slot)

    def ring_sum_1(p, r, w):
        sem = sems.take(6)
        ring_part(p, r, w, sem, range(4))
        return sem

    def ring_sum_2(p, r, w, sem):
        for slot, lanes, dev in ((0, pl.ds(0, w), right), (1, pl.ds(w, w), left)):
            wait_recv(r.at[slot], sem + slot)
            r[6 + slot] = (
                r[slot].astype(F32) + p[chunk(dev), lanes].astype(F32)
            ).astype(BF16)
            rdma(r.at[6 + slot], r.at[4 + slot], sem + 4 + slot, (dev, e)).start()
            note_send(r.at[4 + slot], sem + 4 + slot)

    def ring_sum_3(p, r, w, sem):
        for slot in range(2, 6):
            wait_recv(r.at[slot], sem + slot)
        a = p[chunk(i), :w].astype(F32) + r[2].astype(F32) + r[4].astype(F32)
        b = p[chunk(i), w:].astype(F32) + r[3].astype(F32) + r[5].astype(F32)
        return a, b

    def ring_gather_1(g, w, sem, half):
        for k, dev in ((0, right), (1, left)):
            view = g.at[chunk(i), pl.ds((k if half == 0 else 1 - k) * w, w)]
            rdma(view, view, sem + 2 * half + k, (dev, e)).start()
            note_send(view, sem + 2 * half + k)

    def ring_gather_2(g, w, sem):
        for k, frm, dev in ((0, left, right), (1, right, left)):
            view = g.at[chunk(frm), pl.ds(k * w, w)]
            wait_recv(view, sem + k)
            rdma(view, view, sem + 4 + k, (dev, e)).start()
            note_send(view, sem + 4 + k)

    def ring_near(g, w, sem):
        for k, frm in ((0, left), (1, right)):
            wait_recv(g.at[chunk(frm), pl.ds((1 - k) * w, w)], sem + 2 + k)

    def ring_gather_3(g, w, sem):
        for k in range(2):
            wait_recv(g.at[chunk(opp), pl.ds(k * w, w)], sem + 4 + k)

    tn = fit(2 * ff, 256)
    tf = fit(ff, 256)
    td = fit(dq, 256)

    def gate_up_block(s, at):
        @pl.loop(0, 2 * ff // tn)
        def _(n):
            cols = pl.ds(pl.multiple_of(n * tn, tn), tn)
            pgu[s, at, cols] = jnp.dot(
                recv[0, s, at], wgu[:, cols], preferred_element_type=F32
            ).astype(BF16)

    def d_hidden(s):
        @pl.loop(0, ff // tf)
        def _(n):
            cols = pl.ds(pl.multiple_of(n * tf, tf), tf)
            pdh[s, :, cols] = lax.dot_general(
                recv[1, s], wd[cols, :], CONTRACT_LAST, preferred_element_type=F32
            ).astype(BF16)
        return ring_sum_1(pdh.at[s], rdh.at[s], ff // 2)

    def hidden(s, sem):
        gate, up = ring_sum_3(pgu.at[s], rgu.at[s], ff, sem)
        gate_s[s, 0] = gate
        gate_s[s, 1] = up
        hid[s, chunk(i), :] = (gate * jax.nn.sigmoid(gate) * up).astype(BF16)
        sem = sems.take(6)
        ring_gather_1(hid.at[s], ff // 2, sem, 0)
        ring_gather_1(hid.at[s], ff // 2, sem, 1)
        return sem

    def d_gate_up(s, sem):
        w = ff // 2
        parts = ring_sum_3(pdh.at[s], rdh.at[s], w, sem)
        for k in range(2):
            cols = slice(k * w, (k + 1) * w)
            gate, up, dh = gate_s[s, 0, :, cols], gate_s[s, 1, :, cols], parts[k]
            sig = jax.nn.sigmoid(gate)
            dgu[s, chunk(i), pl.ds(k * w, w)] = (
                dh * up * sig * (1.0 + gate * (1.0 - sig))
            ).astype(BF16)
            dgu[s, chunk(i), pl.ds(ff + k * w, w)] = (dh * (gate * sig)).astype(BF16)
        return sems.take(6)

    def out_rows(s):
        @pl.loop(0, dq // td)
        def _(n):
            cols = pl.ds(pl.multiple_of(n * td, td), td)
            ret_s[0, s, :, cols] = jnp.dot(
                hid[s], wd[:, cols], preferred_element_type=F32
            ).astype(BF16)
        return exchange(ret_s.at[0, s], ret.at[0, s])

    def back_block(s, at):
        @pl.loop(0, dq // td)
        def _(n):
            cols = pl.ds(pl.multiple_of(n * td, td), td)
            ret_s[1, s, at, cols] = lax.dot_general(
                dgu[s, at], wgu[cols, :], CONTRACT_LAST, preferred_element_type=F32
            ).astype(BF16)

    def back_rows(s):
        back_block(s, slice(None))
        return exchange(ret_s.at[1, s], ret.at[1, s])

    def back_send(s, k, back_sem):
        back_block(s, chunk(k))
        for kind in range(2):
            @pl.loop(0, qc)
            def _(n, kind=kind):
                q = k * qc + n
                there, mine = q_rows(kind, q), q_rows(kind, me_q[kind])

                @pl.when(q != me_q[kind])
                def _():
                    rdma(
                        ret_s.at[1, s, there], ret.at[1, s, mine],
                        back_sem, (i, q_dev(kind, q)),
                    ).start()

                @pl.when(q == me_q[kind])
                def _():
                    ret[1, s, mine] = ret_s[1, s, mine]

    def combine(t, s, arrived):
        wait_all(arrived)
        got = ret[t, s]
        if t == 0:
            sums = lax.dot_general(
                whi[s], got, CONTRACT_FIRST, preferred_element_type=F32
            ) + lax.dot_general(wlo[s], got, CONTRACT_FIRST, preferred_element_type=F32)
        else:
            sums = lax.dot_general(dmat[s], got, CONTRACT_FIRST, preferred_element_type=F32)
        part[t, s] = sums.astype(BF16)
        sem = sems.take(1)
        for kind in range(2):
            mine = src_rows(kind, me_src[kind])

            @pl.loop(1, n8)
            def _(k, kind=kind, sem=sem, mine=mine):
                p = (me_src[kind] + k) % n8
                rdma(
                    part.at[t, s, src_rows(kind, p)], psum.at[t, s, mine],
                    sem, (i, src_dev(kind, p)),
                ).start()
            psum[t, s, mine] = part[t, s, mine]
        view = psum.at[t, s, pl.ds(0, 2 * (n8 - 1) * tok)]
        note_send(view, sem)
        return [(view, sem)]

    def finish(t, s, arrived):
        wait_all(arrived)
        for kind in range(2):
            acc = psum[t, s, kind * gt : kind * gt + tok].astype(F32)
            for p in range(1, n8):
                acc = acc + psum[t, s, kind * gt + p * tok : kind * gt + (p + 1) * tok].astype(F32)
            fin[t, 2 * kind + s] = acc.astype(BF16)

    def give_back(t):
        sem = sems.take(1)
        for k in (2, 1, 3):
            peer = (i + k) % xs
            rdma(fin.at[t, peer], land.at[t, i], sem, (peer, e)).start()
        land[t, i] = fin[t, i]
        view = land.at[t, pl.ds(0, xs - 1)]
        note_send(view, sem)
        return view, sem

    stores = []

    def store(src, dst):
        copy = pltpu.make_async_copy(src, dst, osem.at[len(stores)])
        copy.start()
        stores.append(copy)

    def take_back(t, landed, dst):
        wait_recv(*landed)
        for j in range(xs):
            tok_out[t, :, j * dq : (j + 1) * dq] = land[t, j]
        store(tok_out.at[t], dst)

    def grad_down(s):
        @pl.loop(0, ff // tf)
        def _(n):
            cols = pl.ds(pl.multiple_of(n * tf, tf), tf)
            value = lax.dot_general(
                hid[s, :, cols], recv[1, s], CONTRACT_FIRST, preferred_element_type=F32
            )
            if s == 0:
                gdacc[cols, :] = value
            else:
                gd[cols, :] = (gdacc[cols, :] + value).astype(BF16)
        if s == 1:
            store(gd, gd_hbm.at[0])

    def grad_gate_up(s):
        for k, ref, dst in ((0, gg, gg_hbm), (1, gu, gu_hbm)):
            @pl.loop(0, ff // tf)
            def _(n, k=k, ref=ref):
                cols = pl.ds(pl.multiple_of(n * tf, tf), tf)
                both = pl.ds(pl.multiple_of(k * ff + n * tf, tf), tf)
                value = lax.dot_general(
                    recv[0, s], dgu[s, :, both], CONTRACT_FIRST, preferred_element_type=F32
                )
                if s == 0:
                    gacc[:, both] = value
                else:
                    ref[:, cols] = (gacc[:, both] + value).astype(BF16)
            if s == 1:
                store(ref, dst.at[0])

    step = jax.named_scope
    with step("h_wx0"):
        gi0 = gather_info(0)
        wait_recv(xdata.at[0, pl.ds(0, xs - 1)], x_sems[0][1])
        owns[1].wait()
        t0 = gather_data(0, 0)
        t1 = gather_data(0, 1)
    with step("h_sel0"):
        wait_all(gi0)
        selection(0)
    with step("h_rows0"):
        r0 = send_rows(0, 0, t0)
    with step("h_sel1"):
        selection(1)
    with step("h_rows1"):
        r1 = send_rows(0, 1, t1)
    with step("h_wx1"):
        gi1 = gather_info(1)
        wait_recv(xdata.at[1, pl.ds(0, xs - 1)], x_sems[1][1])
        owns[3].wait()
        c0 = gather_data(1, 0)
        c1 = gather_data(1, 1)
    with step("h_wload"):
        loads[0].wait()
        loads[1].wait()
    with step("a_wrow0"):
        wait_all(r0)
    with step("a_gu0"):
        gu_sem = [sems.take(6), sems.take(6)]
        gate_up_block(0, chunk(opp))
        ring_part(pgu.at[0], rgu.at[0], ff, gu_sem[0], (0, 1))
        gate_up_block(0, chunk(left))
        ring_part(pgu.at[0], rgu.at[0], ff, gu_sem[0], (2,))
        gate_up_block(0, chunk(right))
        ring_part(pgu.at[0], rgu.at[0], ff, gu_sem[0], (3,))
        gate_up_block(0, chunk(i))
    with step("a_wrow1"):
        wait_all(r1)
    with step("a_gu1"):
        gate_up_block(1, slice(None))
    with step("a_gu0r2"):
        ring_sum_2(pgu.at[0], rgu.at[0], ff, gu_sem[0])
        ring_part(pgu.at[1], rgu.at[1], ff, gu_sem[1], range(4))
    with step("h_wei"):
        wait_all(gi1)
        weighting(0)
        weighting(1)
    with step("h_dr0"):
        d0 = send_rows(1, 0, c0)
    with step("h_dr1"):
        d1 = send_rows(1, 1, c1)
        loads[2].wait()
    with step("a_hid0"):
        h0 = hidden(0, gu_sem[0])
    with step("a_dh0"):
        wait_all(d0)
        dh0 = d_hidden(0)
    with step("a_gu1r2"):
        ring_sum_2(pgu.at[1], rgu.at[1], ff, gu_sem[1])
    with step("a_dh1"):
        wait_all(d1)
        dh1 = d_hidden(1)
    with step("a_hg0"):
        ring_gather_2(hid.at[0], ff // 2, h0)
    with step("a_hid1"):
        h1 = hidden(1, gu_sem[1])
    with step("a_dh0r2"):
        ring_sum_2(pdh.at[0], rdh.at[0], ff // 2, dh0)
    with step("a_dh1r2"):
        ring_sum_2(pdh.at[1], rdh.at[1], ff // 2, dh1)
    with step("a_out0"):
        ring_near(hid.at[0], ff // 2, h0)
        ring_gather_3(hid.at[0], ff // 2, h0)
        o0 = out_rows(0)
    with step("a_hg1"):
        ring_gather_2(hid.at[1], ff // 2, h1)
    with step("a_dg0"):
        g0 = d_gate_up(0, dh0)
        ring_gather_1(dgu.at[0], ff, g0, 0)
        ring_gather_1(dgu.at[0], ff, g0, 1)
    with step("a_co0"):
        co0 = combine(0, 0, o0)
    with step("a_dg1"):
        g1 = d_gate_up(1, dh1)
    with step("a_wh1"):
        ring_near(hid.at[1], ff // 2, h1)
        ring_gather_3(hid.at[1], ff // 2, h1)
    with step("a_out1"):
        o1 = out_rows(1)
    with step("a_gg0r2"):
        ring_gather_2(dgu.at[0], ff, g0)
        ring_gather_1(dgu.at[1], ff, g1, 0)
        ring_gather_1(dgu.at[1], ff, g1, 1)
    with step("a_gd0"):
        grad_down(0)
    with step("a_gd1"):
        grad_down(1)
    with step("a_fin00"):
        finish(0, 0, co0)
    with step("a_co1"):
        co1 = combine(0, 1, o1)
    with step("a_wg0"):
        ring_near(dgu.at[0], ff, g0)
        ring_gather_3(dgu.at[0], ff, g0)
    with step("a_back0"):
        b0 = back_rows(0)
    with step("a_gg1r2"):
        ring_gather_2(dgu.at[1], ff, g1)
    back_sem = sems.take(1)
    with step("t_bk1own"):
        back_send(1, i, back_sem)
    with step("t_fin01"):
        finish(0, 1, co1)
        land_o = give_back(0)
    with step("t_wnear"):
        ring_near(dgu.at[1], ff, g1)
    with step("t_bk1lr"):
        back_send(1, left, back_sem)
        back_send(1, right, back_sem)
    with step("t_wlast"):
        ring_gather_3(dgu.at[1], ff, g1)
    with step("t_bk1opp"):
        back_send(1, opp, back_sem)
        view = ret.at[1, 1, pl.ds(0, 2 * (nq - 1) * size)]
        note_send(view, back_sem)
        b1 = [(view, back_sem)]
    with step("t_cb0"):
        cb0 = combine(1, 0, b0)
    with step("t_ggu0"):
        grad_gate_up(0)
    with step("t_cb1"):
        cb1 = combine(1, 1, b1)
    with step("t_ggu1"):
        grad_gate_up(1)
    with step("t_tko"):
        take_back(0, land_o, out_hbm)
    with step("t_fb0"):
        finish(1, 0, cb0)
    with step("t_fb1"):
        finish(1, 1, cb1)
        land_b = give_back(1)
    with step("t_tkb"):
        take_back(1, land_b, dtok_hbm)
    with step("t_end"):
        for ref, sem in started:
            rdma(ref, ref, sem, (i, e)).wait_send()
        for copy in stores:
            copy.wait()
    assert sems.count == ssem.shape[0], sems.count


def hand_over(*refs):
    n = len(refs) // 2
    sources, targets, sem = refs[:n], refs[n : 2 * n], refs[2 * n]
    copies = []
    for a in range(n):
        lead = sources[a].shape[0]
        cut = 2 if lead > 64 else 1
        for k in range(cut):
            rows = pl.ds(k * (lead // cut), lead // cut)
            copies.append(
                pltpu.make_async_copy(
                    sources[a].at[rows], targets[a].at[rows], sem.at[len(copies)]
                )
            )
    for copy in copies:
        copy.start()
    for copy in copies:
        copy.wait()


def local(shape, tokens, routes, gates, cotangent, w_gate, w_up, w_down):
    nz, ny, nc = shape
    assert nz == ny
    n8 = nz
    tok, features = tokens.shape
    fanout = routes.shape[1]
    xs = 4
    dq, ff = w_gate.shape[1], w_gate.shape[2]
    total = 2 * n8 * nc * n8 * 2
    blk = total // xs
    gt = n8 * tok
    V = pltpu.VMEM
    nsem = 72
    hb = pl.BlockSpec(memory_space=pl.ANY)
    sds = jax.ShapeDtypeStruct
    shapes = (
        sds((tok, features), BF16), sds((tok, features), BF16),
        sds(w_gate.shape, BF16), sds(w_up.shape, BF16), sds(w_down.shape, BF16),
    )
    pin = lambda v: pltpu.with_memory_space_constraint(v, pltpu.HBM)
    results = pl.pallas_call(
        functools.partial(body, (n8, nc, dq, ff, tok)),
        out_shape=shapes,
        in_specs=[pl.BlockSpec(memory_space=pltpu.HBM)] * 7,
        out_specs=(hb,) * 5,
        scratch_shapes=[
            V((fanout, tok), jnp.int32),
            V((fanout, tok), F32),
            V((fanout, 128), jnp.int32),
            V((fanout, 128), F32),
            V((dq, 2 * ff), BF16),
            V((ff, dq), BF16),
            V((xs, fanout, 128), jnp.int32),
            V((xs, fanout, 128), F32),
            V((2, xs, tok, dq), BF16),
            V((2, n8, 2, fanout, 128), jnp.int32),
            V((2, n8, 2, fanout, 128), F32),
            V((2, 2, 2 * gt, dq), BF16),
            V((2, total, 2 * gt), BF16),
            V((2, total, 2 * gt), BF16),
            V((2, total, 2 * gt), BF16),
            V((2, total, 1), F32),
            V((2, 2, total, dq), BF16),
            V((2, 2, total, dq), BF16),
            V((2, total, 2 * ff), BF16),
            V((2, total, ff), BF16),
            V((2, 8, blk, ff), BF16),
            V((2, 8, blk, ff // 2), BF16),
            V((2, total, ff), BF16),
            V((2, total, 2 * ff), BF16),
            V((2, 2, blk, ff), F32),
            V((dq, 2 * ff), F32),
            V((ff, dq), F32),
            V((2, 2, total, dq), BF16),
            V((2, 2, total, dq), BF16),
            V((2, 2, 2 * gt, dq), BF16),
            V((2, 2, 2 * gt, dq), BF16),
            V((2, xs, tok, dq), BF16),
            V((2, xs, tok, dq), BF16),
            V((dq, ff), BF16),
            V((dq, ff), BF16),
            V((ff, dq), BF16),
            V((2, tok, features), BF16),
            pltpu.SemaphoreType.DMA((7,)),
            pltpu.SemaphoreType.DMA((5,)),
            pltpu.SemaphoreType.DMA((nsem,)),
            pltpu.SemaphoreType.DMA((nsem,)),
        ],
        compiler_params=pltpu.CompilerParams(
            collective_id=0, has_side_effects=True, vmem_limit_bytes=48 * 1024 * 1024
        ),
        name="moe_layer",
    )(*map(pin, (routes.T, gates.T, tokens, cotangent, w_gate, w_up, w_down)))
    flat = [r.reshape(-1, r.shape[-1]) for r in results]
    shapes2 = [sds(r.shape, BF16) for r in flat]
    given = pl.pallas_call(
        hand_over,
        out_shape=shapes2,
        in_specs=[hb] * 5,
        out_specs=[hb] * 5,
        scratch_shapes=[pltpu.SemaphoreType.DMA((16,))],
        compiler_params=pltpu.CompilerParams(vmem_limit_bytes=4 * 1024 * 1024),
        name="hand_over",
    )(*flat)
    return tuple(g.reshape(s.shape) for g, s in zip(given, shapes))


def solution(mesh):
    return jax.shard_map(
        functools.partial(local, LAYOUT[mesh.shape["expert"]]),
        mesh=mesh,
        in_specs=(
            P(("dp", "expert"), None),
            P(("dp", "expert"), None),
            P(("dp", "expert"), None),
            P(("dp", "expert"), None),
            P("expert", "dp", None),
            P("expert", "dp", None),
            P("expert", None, "dp"),
        ),
        out_specs=(
            P(("dp", "expert"), None),
            P(("dp", "expert"), None),
            P("expert", "dp", None),
            P("expert", "dp", None),
            P("expert", None, "dp"),
        ),
        check_vma=False,
    )
```

time: 166 us -> 140 us (0.84)
  Pallas kernels: 156 us -> 139 us
  local copies, waits for them, and re-layouts: 7.94 us -> 0 us
    pallas_call x1 -> x2, Pallas kernels: 156 us -> 139 us  [the longest x1 138 us: local(): pl.pallas_call(functools.partial(body, (n8, nc, dq, ff, tok)), out_shape=...]
    unnamed x13 -> x0, local copies, waits for them, and re-layouts: 6.59 us -> none
where the time goes in v2:
time: 140 us
  Pallas kernels  139 us (99%)
    pallas_call x1, Pallas kernels, local(): pl.pallas_call(functools.partial(body, (n8, nc, dq, ff, tok)), out_shape=...  138 us

profile of v2, /device:TPU:1, one launch (start us, length us, event | category | flops | bytes accessed | tf_op | source)
XLA Modules:
  0.0 139.8 jit_solution(17949153236872721676)
XLA Ops:
  0.6 137.6 %moe_layer.1 = (bf16[16,2048]{1,0:T(8,128)(2,1)S(1)}, bf16[16,2048]{1,0:T(8,128)(2,1)S(1)}, bf16[1,512,768]{2,1,0:T(8,128)(2,1)S(1)}, bf16[1,512,768]{2,1,0:T(8,128)(2,1)S(1)}, bf16[1,768,512]{2,1,0:T(8,128)(2,1)S(1)}) custom-call(s32[8,16]{1,0:T(8,128)} %bitcast.11, f32[8,16]{1,0:T(8,128)} %bitcast.12, bf16[16,2048]{1,0:T(8,128)(2,1)} %tok_ref.1, ...), custom_call_target="tpu_custom_call" | custom-call | tf_op jit(solution)/shard_map/moe_layer/pallas_call | solution.py:654
  138.3 1.6 %hand_over.1 = (bf16[16,2048]{1,0:T(8,128)(2,1)}, bf16[16,2048]{1,0:T(8,128)(2,1)}, bf16[512,768]{1,0:T(8,128)(2,1)}, bf16[512,768]{1,0:T(8,128)(2,1)}, bf16[768,512]{1,0:T(8,128)(2,1)}) custom-call(bf16[16,2048]{1,0:T(8,128)(2,1)S(1)} %get-tuple-element.15.refs_0_, bf16[16,2048]{1,0:T(8,128)(2,1)S(1)} %get-tuple-element.16.refs_1_, ...), custom_call_target="tpu_custom_call" | custom-call | tf_op jit(solution)/shard_map/hand_over/pallas_call | solution.py:709

commit v3 on v2

v3 whole, which is shorter than its diff:
```python
import functools

import jax
import jax.numpy as jnp
from jax import lax
from jax.experimental import pallas as pl
from jax.experimental.pallas import tpu as pltpu
from jax.sharding import PartitionSpec as P

MESH = pl.DeviceIdType.MESH
LAYOUT = {128: (8, 8, 2), 8: (2, 2, 2)}
F32, BF16 = jnp.float32, jnp.bfloat16
CONTRACT_LAST = (((1,), (1,)), ((), ()))
CONTRACT_FIRST = (((0,), (0,)), ((), ()))


def fit(total, want):
    return want if total % want == 0 else total


class Sems:
    def __init__(self):
        self.count = 0

    def take(self, n=1):
        first = self.count
        self.count += n
        return first


def body(
    cfg,
    routes_ref, gates_ref, tok_ref, cot_ref, wg_hbm, wu_hbm, wd_hbm,
    out_hbm, dtok_hbm, gg_hbm, gu_hbm, gd_hbm,
    raw_r, raw_g, own_r, own_g, wgu, wd, xroutes, xgates, xdata, groutes, ggates, gdata,
    dmat, whi, wlo, gcol, rows, recv, pgu, pdh, rgu, rdh, hid, dgu, gate_s, gacc, gdacc,
    ret_s, ret, part, psum, fin, land, gg, gu, gd, tok_out,
    wsem, osem, ssem, rsem,
):
    n8, nc, dq, ff, tok = cfg
    xs = 4
    nq = n8 * nc
    size = 2 * n8
    total = nq * size
    per = nq // xs
    blk = per * size
    gt = n8 * tok
    i = lax.axis_index("dp")
    e = lax.axis_index("expert")
    z, yc = e // nq, e % nq
    y, c = yc // nc, yc % nc
    right, left, opp = (i + 1) % xs, (i + 3) % xs, (i + 2) % xs
    sends, recvs = Sems(), Sems()

    def pick(kind, a, b):
        return jnp.where(kind == 0, a, b)

    me_src = pick(c, z, y)
    me_q = pick(c, yc, z * nc + c)

    def src_dev(p):
        return pick(c, (p * n8 + y) * nc, (z * n8 + p) * nc + 1)

    def q_dev(q):
        return pick(c, z * nq + q, ((q // nc) * n8 + y) * nc + q % nc)

    def block(p):
        return pl.ds(p * size if isinstance(p, int) else pl.multiple_of(p * size, size), size)

    def src_rows(p):
        return pl.ds(pl.multiple_of(p * tok, tok), tok)

    def rdma(src, dst, ss, rs, dev):
        return pltpu.make_async_remote_copy(
            src_ref=src, dst_ref=dst, send_sem=ssem.at[ss], recv_sem=rsem.at[rs],
            device_id=dev, device_id_type=MESH,
        )

    started = []

    def wait_recv(ref, sem):
        rdma(ref, ref, 0, sem, (i, e)).wait_recv()

    def note_send(ref, sem):
        started.append((ref, sem))

    shared = {}

    def send_group(name, view):
        if name not in shared:
            shared[name] = sends.take()
            note_send(view, shared[name])
        return shared[name]

    part_of = lambda ref, k: ref.at[:, pl.ds(pl.multiple_of(k * dq, 128), dq)]
    owns = [
        pltpu.make_async_copy(routes_ref, raw_r, wsem.at[3]),
        pltpu.make_async_copy(part_of(tok_ref, i), xdata.at[0, i], wsem.at[4]),
        pltpu.make_async_copy(gates_ref, raw_g, wsem.at[5]),
        pltpu.make_async_copy(part_of(cot_ref, i), xdata.at[1, i], wsem.at[6]),
    ]
    for own in owns:
        own.start()
    loads = [
        pltpu.make_async_copy(wg_hbm.at[0], wgu.at[:, pl.ds(0, ff)], wsem.at[0]),
        pltpu.make_async_copy(wu_hbm.at[0], wgu.at[:, pl.ds(ff, ff)], wsem.at[1]),
        pltpu.make_async_copy(wd_hbm.at[0], wd, wsem.at[2]),
    ]
    for load in loads:
        load.start()

    with jax.named_scope("h_barrier"):
        barrier = pltpu.get_barrier_semaphore()
        for k in range(1, xs):
            pl.semaphore_signal(barrier, inc=1, device_id=((i + k) % xs, e), device_id_type=MESH)

        @pl.loop(1, nq)
        def _(k):
            peer = z * nq + (yc + k) % nq
            pl.semaphore_signal(barrier, inc=1, device_id=(i, peer), device_id_type=MESH)
            q = (z * nc + c + k) % nq
            peer = ((q // nc) * n8 + y) * nc + q % nc
            pl.semaphore_signal(barrier, inc=1, device_id=(i, peer), device_id_type=MESH)
        for t, raw, tile_ref in ((0, raw_r, own_r), (1, raw_g, own_g)):
            owns[2 * t].wait()
            value = raw[...]
            blank = jnp.zeros((value.shape[0], 128 - tok), value.dtype)
            tile_ref[...] = jnp.concatenate([value, blank], axis=1)
        pl.semaphore_wait(barrier, xs - 1 + 2 * (nq - 1))

    info = ((own_r, xroutes, groutes), (own_g, xgates, ggates))
    data_refs = (tok_ref, cot_ref)
    x_sems = []
    with jax.named_scope("h_x"):
        for t in range(2):
            own, xinfo, _ = info[t]
            x_sems.append((recvs.take(), recvs.take()))
            si, sd = sends.take(), sends.take()
            for k in (2, 1, 3):
                peer = (i + k) % xs
                rdma(own, xinfo.at[i], si, x_sems[t][0], (peer, e)).start()
                rdma(
                    part_of(data_refs[t], peer), xdata.at[t, i], sd, x_sems[t][1], (peer, e)
                ).start()
            xinfo[i] = own[...]
            note_send(xinfo.at[pl.ds(0, xs - 1)], si)
            note_send(xdata.at[t, pl.ds(0, xs - 1)], sd)

    def split_ready(t):
        wait_recv(info[t][1].at[pl.ds(0, xs - 1)], x_sems[t][0])
        wait_recv(xdata.at[t, pl.ds(0, xs - 1)], x_sems[t][1])
        owns[2 * t + 1].wait()

    def gather(t, s):
        got = []
        _, xinfo, ginfo = info[t]
        tiles, feats = pl.ds(0, n8 - 1), pl.ds(0, (n8 - 1) * tok)
        for src, dst, view, ss in (
            (
                xinfo.at[s], ginfo.at[s, me_src], ginfo.at[s, tiles],
                send_group(("info", t), ginfo.at[:, tiles]),
            ),
            (
                xdata.at[t, s], gdata.at[t, s, src_rows(me_src)], gdata.at[t, s, feats],
                send_group(("data", t), gdata.at[t, :, feats]),
            ),
        ):
            rs = recvs.take()

            @pl.loop(1, n8)
            def _(k, src=src, dst=dst, ss=ss, rs=rs):
                rdma(src, dst, ss, rs, (i, src_dev((me_src + k) % n8))).start()
            dst[...] = src[...]
            got.append((view, rs))
        return got

    def wait_all(pairs):
        for view, sem in pairs:
            wait_recv(view, sem)

    others = pl.ds(0, (nq - 1) * size)

    def slots_out(t, s):
        src, dst = rows.at[t, s], recv.at[t, s]
        ss, rs = send_group(("out", t), recv.at[t, :, others]), recvs.take()
        mine = block(2 * pick(c, y, z) + c)

        @pl.loop(1, nq)
        def _(k):
            q = (me_q + k) % nq
            rdma(src.at[block(q)], dst.at[mine], ss, rs, (i, q_dev(q))).start()
        dst[mine] = src[block(me_q)]
        return [(dst.at[others], rs)]

    def slots_back(src, dst, first, count, ss, rs):
        @pl.loop(0, count)
        def _(n):
            p = first + n
            kind, at = p % 2, p // 2
            dev = pick(kind, z * nq + at * nc, (at * n8 + y) * nc + 1)
            there = block(pick(kind, yc, z * nc + c))

            @pl.when(dev != e)
            def _():
                rdma(src.at[block(p)], dst.at[there], ss, rs, (i, dev)).start()

            @pl.when(dev == e)
            def _():
                dst[there] = src[block(p)]

    def tile(ginfo, s):
        return jnp.concatenate([ginfo[s, p][:, :tok] for p in range(n8)], axis=1)

    def matches(s):
        names = tile(groutes, s)
        wanted = q_dev(lax.broadcasted_iota(jnp.int32, (nq, gt), 0))
        return [names[k : k + 1] == wanted for k in range(names.shape[0])]

    before_r = lax.broadcasted_iota(jnp.int32, (gt, gt), 0)
    before_c = lax.broadcasted_iota(jnp.int32, (gt, gt), 1)
    earlier = jnp.where(
        (before_r // tok == before_c // tok) & (before_r < before_c), 1.0, 0.0
    ).astype(BF16)
    slot_r = lax.broadcasted_iota(jnp.int32, (size, gt), 0)
    cell = lax.broadcasted_iota(jnp.int32, (size, gt), 1) // tok == slot_r // 2
    seg0 = jnp.where(cell & (slot_r % 2 == 0), 1.0, 0.0)
    seg1 = jnp.where(cell & (slot_r % 2 == 1), 1.0, 0.0)

    def selection(s):
        hit = jnp.zeros((nq, gt), F32)
        for m in matches(s):
            hit = jnp.where(m, 1.0, hit)
        prior = jnp.dot(hit.astype(BF16), earlier, preferred_element_type=F32)
        first = jnp.where(prior < 0.5, hit, 0.0)
        second = hit - first
        for q in range(nq):
            dmat[s, block(q), :] = (
                seg0 * first[q : q + 1] + seg1 * second[q : q + 1]
            ).astype(BF16)

    def weighting(s):
        values = tile(ggates, s)
        gate = jnp.zeros((nq, gt), F32)
        for k, m in enumerate(matches(s)):
            gate = jnp.where(m, values[k : k + 1], gate)
        for q in range(nq):
            w = dmat[s, block(q), :].astype(F32) * gate[q : q + 1]
            hi = w.astype(BF16)
            whi[s, block(q), :] = hi
            wlo[s, block(q), :] = (w - hi.astype(F32)).astype(BF16)
            gcol[s, block(q), :] = jnp.sum(w, axis=1, keepdims=True)

    def send_rows(t, s):
        picked = jnp.dot(dmat[s], gdata[t, s], preferred_element_type=F32)
        if t == 1:
            picked = picked * gcol[s]
        rows[t, s] = picked.astype(BF16)
        return slots_out(t, s)

    def chunk(k):
        return pl.ds(pl.multiple_of(k * blk, blk), blk)

    def ring_sum_open(name, r):
        return send_group(name, r.at[:, pl.ds(0, 6)]), recvs.take(3)

    def ring_sum_1(p, r, w, sem, slots):
        ss, rs = sem
        a, b = pl.ds(0, w), pl.ds(w, w)
        for slot in slots:
            at, lanes, dev = (
                (opp, a, right), (opp, b, left), (left, a, left), (right, b, right)
            )[slot]
            rdma(
                p.at[chunk(at), lanes], r.at[slot], ss, rs + min(slot, 2), (dev, e)
            ).start()

    def ring_sum_2(p, r, w, sem):
        ss, rs = sem
        for slot, lanes, dev in ((0, pl.ds(0, w), right), (1, pl.ds(w, w), left)):
            wait_recv(r.at[slot], rs + slot)
            r[6 + slot] = (
                r[slot].astype(F32) + p[chunk(dev), lanes].astype(F32)
            ).astype(BF16)
            rdma(r.at[6 + slot], r.at[4 + slot], ss, rs + 2, (dev, e)).start()

    def ring_sum_3(p, r, w, sem):
        wait_recv(r.at[pl.ds(2, 4)], sem[1] + 2)
        a = p[chunk(i), :w].astype(F32) + r[2].astype(F32) + r[4].astype(F32)
        b = p[chunk(i), w:].astype(F32) + r[3].astype(F32) + r[5].astype(F32)
        return a, b

    def ring_gather_open(name, whole):
        return send_group(name, whole.at[:, pl.ds(0, 3 * blk)]), recvs.take(4)

    def ring_gather_1(g, w, sem, half):
        ss, rs = sem
        for k, dev in ((0, right), (1, left)):
            view = g.at[chunk(i), pl.ds((k if half == 0 else 1 - k) * w, w)]
            rdma(view, view, ss, rs + (k if half == 0 else 2), (dev, e)).start()

    def ring_gather_2(g, w, sem):
        ss, rs = sem
        for k, frm, dev in ((0, left, right), (1, right, left)):
            view = g.at[chunk(frm), pl.ds(k * w, w)]
            wait_recv(view, rs + k)
            rdma(view, view, ss, rs + 3, (dev, e)).start()

    def ring_near(g, sem):
        wait_recv(g.at[chunk(left)], sem[1] + 2)

    def ring_gather_3(g, sem):
        wait_recv(g.at[chunk(opp)], sem[1] + 3)

    tf = fit(ff, 256)
    td = fit(dq, 256)

    def gate_up(s):
        ring = ring_sum_open("gu", rgu)
        for k in range(2):
            @pl.loop(0, ff // tf)
            def _(n, k=k):
                cols = pl.ds(pl.multiple_of(k * ff + n * tf, tf), tf)
                pgu[s, :, cols] = jnp.dot(
                    recv[0, s], wgu[:, cols], preferred_element_type=F32
                ).astype(BF16)
            ring_sum_1(pgu.at[s], rgu.at[s], ff, ring, (0, 2) if k == 0 else (1, 3))
        return ring

    def d_hidden(s):
        @pl.loop(0, ff // tf)
        def _(n):
            cols = pl.ds(pl.multiple_of(n * tf, tf), tf)
            pdh[s, :, cols] = lax.dot_general(
                recv[1, s], wd[cols, :], CONTRACT_LAST, preferred_element_type=F32
            ).astype(BF16)
        ring = ring_sum_open("dh", rdh)
        ring_sum_1(pdh.at[s], rdh.at[s], ff // 2, ring, range(4))
        return ring

    def hidden(s, sem):
        gate, up = ring_sum_3(pgu.at[s], rgu.at[s], ff, sem)
        gate_s[s, 0] = gate
        gate_s[s, 1] = up
        hid[s, chunk(i), :] = (gate * jax.nn.sigmoid(gate) * up).astype(BF16)
        ring = ring_gather_open("hid", hid)
        ring_gather_1(hid.at[s], ff // 2, ring, 0)
        ring_gather_1(hid.at[s], ff // 2, ring, 1)
        return ring

    def d_gate_up(s, sem):
        w = ff // 2
        parts = ring_sum_3(pdh.at[s], rdh.at[s], w, sem)
        for k in range(2):
            cols = slice(k * w, (k + 1) * w)
            gate, up, dh = gate_s[s, 0, :, cols], gate_s[s, 1, :, cols], parts[k]
            sig = jax.nn.sigmoid(gate)
            dgu[s, chunk(i), pl.ds(k * w, w)] = (
                dh * up * sig * (1.0 + gate * (1.0 - sig))
            ).astype(BF16)
            dgu[s, chunk(i), pl.ds(ff + k * w, w)] = (dh * (gate * sig)).astype(BF16)
        ring = ring_gather_open("dgu", dgu)
        ring_gather_1(dgu.at[s], ff, ring, 0)
        return ring

    def back_open(t):
        return send_group(("ret", t), ret.at[t, :, others]), recvs.take()

    def all_back(t, s):
        ss, rs = back_open(t)
        slots_back(ret_s.at[t, s], ret.at[t, s], 0, nq, ss, rs)
        return [(ret.at[t, s, others], rs)]

    def out_rows(s):
        @pl.loop(0, dq // td)
        def _(n):
            cols = pl.ds(pl.multiple_of(n * td, td), td)
            ret_s[0, s, :, cols] = jnp.dot(
                hid[s], wd[:, cols], preferred_element_type=F32
            ).astype(BF16)
        return all_back(0, s)

    def back_block(s, at):
        @pl.loop(0, dq // td)
        def _(n):
            cols = pl.ds(pl.multiple_of(n * td, td), td)
            ret_s[1, s, at, cols] = lax.dot_general(
                dgu[s, at], wgu[cols, :], CONTRACT_LAST, preferred_element_type=F32
            ).astype(BF16)

    def back_rows(s):
        back_block(s, slice(None))
        return all_back(1, s)

    def back_send(s, k, sem):
        back_block(s, chunk(k))
        slots_back(ret_s.at[1, s], ret.at[1, s], k * per, per, *sem)

    def combine(t, s, arrived):
        wait_all(arrived)
        got = ret[t, s]
        if t == 0:
            sums = lax.dot_general(
                whi[s], got, CONTRACT_FIRST, preferred_element_type=F32
            ) + lax.dot_general(wlo[s], got, CONTRACT_FIRST, preferred_element_type=F32)
        else:
            sums = lax.dot_general(dmat[s], got, CONTRACT_FIRST, preferred_element_type=F32)
        part[t, s] = sums.astype(BF16)
        feats = pl.ds(0, (n8 - 1) * tok)
        ss, rs = send_group(("sum", t), psum.at[t, :, feats]), recvs.take()
        mine = src_rows(me_src)

        @pl.loop(1, n8)
        def _(k):
            p = (me_src + k) % n8
            rdma(
                part.at[t, s, src_rows(p)], psum.at[t, s, mine], ss, rs, (i, src_dev(p))
            ).start()
        psum[t, s, mine] = part[t, s, mine]
        return [(psum.at[t, s, feats], rs)]

    def finish(t, s, arrived):
        wait_all(arrived)
        acc = psum[t, s, :tok].astype(F32)
        for p in range(1, n8):
            acc = acc + psum[t, s, p * tok : (p + 1) * tok].astype(F32)
        fin[t, s] = acc.astype(BF16)

    def give_back(t):
        ss, rs = sends.take(), recvs.take()
        for k in (2, 1, 3):
            peer = (i + k) % xs
            rdma(fin.at[t, peer], land.at[t, i], ss, rs, (peer, e)).start()
        land[t, i] = fin[t, i]
        view = land.at[t, pl.ds(0, xs - 1)]
        note_send(view, ss)
        return view, rs

    stores = []

    def store(src, dst):
        copy = pltpu.make_async_copy(src, dst, osem.at[len(stores)])
        copy.start()
        stores.append(copy)

    def take_back(t, landed, dst):
        wait_recv(*landed)
        for j in range(xs):
            tok_out[t, :, j * dq : (j + 1) * dq] = land[t, j]
        store(tok_out.at[t], dst)

    def pair(ref, p, cols):
        both = ref[2 * p : 2 * p + 2, :, cols]
        return both.reshape(2 * total, both.shape[-1])

    def grad_down(p):
        @pl.loop(0, ff // tf)
        def _(n):
            cols = pl.ds(pl.multiple_of(n * tf, tf), tf)
            value = lax.dot_general(
                pair(hid, p, cols), pair(recv.at[1], p, slice(None)), CONTRACT_FIRST,
                preferred_element_type=F32,
            )
            if p == 0:
                gdacc[cols, :] = value
            else:
                gd[cols, :] = (gdacc[cols, :] + value).astype(BF16)
        if p == 1:
            store(gd, gd_hbm.at[0])

    def grad_gate_up(p):
        for k, ref, dst in ((0, gg, gg_hbm), (1, gu, gu_hbm)):
            @pl.loop(0, ff // tf)
            def _(n, k=k, ref=ref):
                cols = pl.ds(pl.multiple_of(n * tf, tf), tf)
                both = pl.ds(pl.multiple_of(k * ff + n * tf, tf), tf)
                value = lax.dot_general(
                    pair(recv.at[0], p, slice(None)), pair(dgu, p, both), CONTRACT_FIRST,
                    preferred_element_type=F32,
                )
                if p == 0:
                    gacc[:, both] = value
                else:
                    ref[:, cols] = (gacc[:, both] + value).astype(BF16)
            if p == 1:
                store(ref, dst.at[0])

    step = jax.named_scope
    r, d, u, v, h, g, o, b, co, cb = ([None] * xs for _ in range(10))
    tg, cg = [None] * xs, [None] * xs

    def token_rows(s):
        with step(f"h_sel{s}"):
            wait_recv(*tg[s][0])
            selection(s)
        with step(f"h_rows{s}"):
            wait_recv(*tg[s][1])
            r[s] = send_rows(0, s)

    def cotangent_rows(s):
        with step(f"h_cot{s}"):
            wait_all(cg[s])
            weighting(s)
            d[s] = send_rows(1, s)

    def do_gu(s):
        with step(f"a_wr{s}"):
            wait_all(r[s])
        with step(f"a_gu{s}"):
            u[s] = gate_up(s)

    def do_gu2(s):
        with step(f"a_gur{s}"):
            ring_sum_2(pgu.at[s], rgu.at[s], ff, u[s])

    def do_hid(s):
        with step(f"a_hid{s}"):
            h[s] = hidden(s, u[s])

    def do_hid2(s):
        with step(f"a_hf{s}"):
            ring_gather_2(hid.at[s], ff // 2, h[s])

    def do_dh(s):
        with step(f"a_dh{s}"):
            wait_all(d[s])
            v[s] = d_hidden(s)

    def do_dh2(s):
        with step(f"a_dhr{s}"):
            ring_sum_2(pdh.at[s], rdh.at[s], ff // 2, v[s])

    def do_dg(s):
        with step(f"a_dg{s}"):
            g[s] = d_gate_up(s, v[s])
            if s == 0:
                ring_gather_1(dgu.at[s], ff, g[s], 1)

    def do_dg2(s):
        with step(f"a_dgf{s}"):
            ring_gather_2(dgu.at[s], ff, g[s])
            if s < xs - 1:
                ring_gather_1(dgu.at[s + 1], ff, g[s + 1], 1)

    def do_out(s):
        with step(f"a_wh{s}"):
            ring_near(hid.at[s], h[s])
            ring_gather_3(hid.at[s], h[s])
        with step(f"a_out{s}"):
            o[s] = out_rows(s)

    def do_back(s):
        with step(f"a_wg{s}"):
            ring_near(dgu.at[s], g[s])
            ring_gather_3(dgu.at[s], g[s])
        with step(f"a_back{s}"):
            b[s] = back_rows(s)

    def do_co(s):
        with step(f"a_co{s}"):
            co[s] = combine(0, s, o[s])

    def do_cb(s):
        with step(f"t_cb{s}"):
            cb[s] = combine(1, s, b[s])

    def do_fin(t, s):
        with step(f"t_fin{t}{s}"):
            finish(t, s, (co, cb)[t][s])

    with step("h_wx0"):
        split_ready(0)
        for s in range(3):
            tg[s] = gather(0, s)
    token_rows(0)
    tg[3] = gather(0, 3)
    token_rows(1)
    token_rows(2)
    loads[0].wait()
    loads[1].wait()
    do_gu(0)
    token_rows(3)
    do_gu(1)
    with step("h_gcot"):
        split_ready(1)
        for s in range(xs):
            cg[s] = gather(1, s)
    do_gu2(0)
    do_gu(2)
    cotangent_rows(0)
    do_gu2(1)
    do_hid(0)
    do_gu(3)
    do_gu2(2)
    do_hid(1)
    do_hid2(0)
    cotangent_rows(1)
    loads[2].wait()
    do_dh(0)
    do_gu2(3)
    do_hid(2)
    do_hid2(1)
    cotangent_rows(2)
    do_dh(1)
    do_dh2(0)
    cotangent_rows(3)
    do_out(0)
    do_hid(3)
    do_hid2(2)
    do_dh(2)
    do_dh2(1)
    do_out(1)
    do_dh(3)
    do_hid2(3)
    do_dh2(2)
    do_dg(0)
    do_out(2)
    do_dh2(3)
    do_dg(1)
    do_co(0)
    do_out(3)
    do_dg2(0)
    do_dg(2)
    do_co(1)
    with step("a_gd0"):
        grad_down(0)
    do_dg2(1)
    do_dg(3)
    do_co(2)
    with step("a_gd1"):
        grad_down(1)
    do_fin(0, 0)
    do_back(0)
    do_dg2(2)
    do_co(3)
    do_fin(0, 1)
    do_back(1)
    do_dg2(3)
    do_cb(0)
    do_fin(0, 2)
    do_back(2)
    sem3 = back_open(1)
    with step("t_bk3own"):
        back_send(3, i, sem3)
    do_cb(1)
    with step("t_wnear"):
        ring_near(dgu.at[3], g[3])
    with step("t_bk3lr"):
        back_send(3, left, sem3)
        back_send(3, right, sem3)
    do_fin(0, 3)
    with step("t_wlast"):
        ring_gather_3(dgu.at[3], g[3])
    with step("t_bk3opp"):
        back_send(3, opp, sem3)
        b[3] = [(ret.at[1, 3, others], sem3[1])]
    with step("t_ggu0"):
        grad_gate_up(0)
    do_cb(2)
    with step("t_give0"):
        land_o = give_back(0)
    do_cb(3)
    with step("t_ggu1"):
        grad_gate_up(1)
    with step("t_tko"):
        take_back(0, land_o, out_hbm)
    for s in range(xs):
        do_fin(1, s)
    with step("t_give1"):
        land_b = give_back(1)
    with step("t_tkb"):
        take_back(1, land_b, dtok_hbm)
    with step("t_end"):
        for ref, sem in started:
            rdma(ref, ref, sem, 0, (i, e)).wait_send()
        for copy in stores:
            copy.wait()
    assert (sends.count, recvs.count) == (ssem.shape[0], rsem.shape[0]), (
        sends.count, recvs.count
    )


def hand_over(*refs):
    n = len(refs) // 2
    sources, targets, sem = refs[:n], refs[n : 2 * n], refs[2 * n]
    copies = []
    for a in range(n):
        lead = sources[a].shape[0]
        cut = 2 if lead > 64 else 1
        for k in range(cut):
            rows = pl.ds(k * (lead // cut), lead // cut)
            copies.append(
                pltpu.make_async_copy(
                    sources[a].at[rows], targets[a].at[rows], sem.at[len(copies)]
                )
            )
    for copy in copies:
        copy.start()
    for copy in copies:
        copy.wait()


def local(shape, tokens, routes, gates, cotangent, w_gate, w_up, w_down):
    nz, ny, nc = shape
    assert nz == ny
    n8 = nz
    tok, features = tokens.shape
    fanout = routes.shape[1]
    xs = 4
    dq, ff = w_gate.shape[1], w_gate.shape[2]
    total = n8 * nc * n8 * 2
    blk = total // xs
    gt = n8 * tok
    V = pltpu.VMEM
    hb = pl.BlockSpec(memory_space=pl.ANY)
    sds = jax.ShapeDtypeStruct
    shapes = (
        sds((tok, features), BF16), sds((tok, features), BF16),
        sds(w_gate.shape, BF16), sds(w_up.shape, BF16), sds(w_down.shape, BF16),
    )
    pin = lambda v: pltpu.with_memory_space_constraint(v, pltpu.HBM)
    results = pl.pallas_call(
        functools.partial(body, (n8, nc, dq, ff, tok)),
        out_shape=shapes,
        in_specs=[pl.BlockSpec(memory_space=pltpu.HBM)] * 7,
        out_specs=(hb,) * 5,
        scratch_shapes=[
            V((fanout, tok), jnp.int32),
            V((fanout, tok), F32),
            V((fanout, 128), jnp.int32),
            V((fanout, 128), F32),
            V((dq, 2 * ff), BF16),
            V((ff, dq), BF16),
            V((xs, fanout, 128), jnp.int32),
            V((xs, fanout, 128), F32),
            V((2, xs, tok, dq), BF16),
            V((xs, n8, fanout, 128), jnp.int32),
            V((xs, n8, fanout, 128), F32),
            V((2, xs, gt, dq), BF16),
            V((xs, total, gt), BF16),
            V((xs, total, gt), BF16),
            V((xs, total, gt), BF16),
            V((xs, total, 1), F32),
            V((2, xs, total, dq), BF16),
            V((2, xs, total, dq), BF16),
            V((xs, total, 2 * ff), BF16),
            V((xs, total, ff), BF16),
            V((xs, 8, blk, ff), BF16),
            V((xs, 8, blk, ff // 2), BF16),
            V((xs, total, ff), BF16),
            V((xs, total, 2 * ff), BF16),
            V((xs, 2, blk, ff), F32),
            V((dq, 2 * ff), F32),
            V((ff, dq), F32),
            V((2, xs, total, dq), BF16),
            V((2, xs, total, dq), BF16),
            V((2, xs, gt, dq), BF16),
            V((2, xs, gt, dq), BF16),
            V((2, xs, tok, dq), BF16),
            V((2, xs, tok, dq), BF16),
            V((dq, ff), BF16),
            V((dq, ff), BF16),
            V((ff, dq), BF16),
            V((2, tok, features), BF16),
            pltpu.SemaphoreType.DMA((7,)),
            pltpu.SemaphoreType.DMA((5,)),
            pltpu.SemaphoreType.DMA((20,)),
            pltpu.SemaphoreType.DMA((102,)),
        ],
        compiler_params=pltpu.CompilerParams(
            collective_id=0, has_side_effects=True, vmem_limit_bytes=48 * 1024 * 1024
        ),
        name="moe_layer",
    )(*map(pin, (routes.T, gates.T, tokens, cotangent, w_gate, w_up, w_down)))
    flat = [r.reshape(-1, r.shape[-1]) for r in results]
    shapes2 = [sds(r.shape, BF16) for r in flat]
    given = pl.pallas_call(
        hand_over,
        out_shape=shapes2,
        in_specs=[hb] * 5,
        out_specs=[hb] * 5,
        scratch_shapes=[pltpu.SemaphoreType.DMA((16,))],
        compiler_params=pltpu.CompilerParams(vmem_limit_bytes=4 * 1024 * 1024),
        name="hand_over",
    )(*flat)
    return tuple(g.reshape(s.shape) for g, s in zip(given, shapes))


def solution(mesh):
    return jax.shard_map(
        functools.partial(local, LAYOUT[mesh.shape["expert"]]),
        mesh=mesh,
        in_specs=(
            P(("dp", "expert"), None),
            P(("dp", "expert"), None),
            P(("dp", "expert"), None),
            P(("dp", "expert"), None),
            P("expert", "dp", None),
            P("expert", "dp", None),
            P("expert", None, "dp"),
        ),
        out_specs=(
            P(("dp", "expert"), None),
            P(("dp", "expert"), None),
            P("expert", "dp", None),
            P("expert", "dp", None),
            P("expert", None, "dp"),
        ),
        check_vma=False,
    )
```

time: 140 us -> 129 us (0.921)
  Pallas kernels: 139 us -> 129 us
    pallas_call x1, Pallas kernels: 138 us -> 127 us  [local(): pl.pallas_call(functools.partial(body, (n8, nc, dq, ff, tok)), out_shape=...]
where the time goes in v3:
time: 129 us
  Pallas kernels  129 us (100%)
    pallas_call x1, Pallas kernels, local(): pl.pallas_call(functools.partial(body, (n8, nc, dq, ff, tok)), out_shape=...  127 us

profile of v3, /device:TPU:1, one launch (start us, length us, event | category | flops | bytes accessed | tf_op | source)
XLA Modules:
  0.0 129.1 jit_solution(5687252999718302084)
XLA Ops:
  0.6 126.9 %moe_layer.1 = (bf16[16,2048]{1,0:T(8,128)(2,1)S(1)}, bf16[16,2048]{1,0:T(8,128)(2,1)S(1)}, bf16[1,512,768]{2,1,0:T(8,128)(2,1)S(1)}, bf16[1,512,768]{2,1,0:T(8,128)(2,1)S(1)}, bf16[1,768,512]{2,1,0:T(8,128)(2,1)S(1)}) custom-call(s32[8,16]{1,0:T(8,128)} %bitcast.11, f32[8,16]{1,0:T(8,128)} %bitcast.12, bf16[16,2048]{1,0:T(8,128)(2,1)} %tok_ref.1, ...), custom_call_target="tpu_custom_call" | custom-call | tf_op jit(solution)/shard_map/moe_layer/pallas_call | solution.py:721
  127.6 1.6 %hand_over.1 = (bf16[16,2048]{1,0:T(8,128)(2,1)}, bf16[16,2048]{1,0:T(8,128)(2,1)}, bf16[512,768]{1,0:T(8,128)(2,1)}, bf16[512,768]{1,0:T(8,128)(2,1)}, bf16[768,512]{1,0:T(8,128)(2,1)}) custom-call(bf16[16,2048]{1,0:T(8,128)(2,1)S(1)} %get-tuple-element.15.refs_0_, bf16[16,2048]{1,0:T(8,128)(2,1)S(1)} %get-tuple-element.16.refs_1_, ...), custom_call_target="tpu_custom_call" | custom-call | tf_op jit(solution)/shard_map/hand_over/pallas_call | solution.py:776

commit v4 on v3

--- a/solution.py
+++ b/solution.py
@@ -99,15 +99,11 @@
         pltpu.make_async_copy(gates_ref, raw_g, wsem.at[5]),
         pltpu.make_async_copy(part_of(cot_ref, i), xdata.at[1, i], wsem.at[6]),
     ]
-    for own in owns:
-        own.start()
     loads = [
         pltpu.make_async_copy(wg_hbm.at[0], wgu.at[:, pl.ds(0, ff)], wsem.at[0]),
         pltpu.make_async_copy(wu_hbm.at[0], wgu.at[:, pl.ds(ff, ff)], wsem.at[1]),
         pltpu.make_async_copy(wd_hbm.at[0], wd, wsem.at[2]),
     ]
-    for load in loads:
-        load.start()
 
     with jax.named_scope("h_barrier"):
         barrier = pltpu.get_barrier_semaphore()
@@ -121,11 +117,8 @@
             q = (z * nc + c + k) % nq
             peer = ((q // nc) * n8 + y) * nc + q % nc
             pl.semaphore_signal(barrier, inc=1, device_id=(i, peer), device_id_type=MESH)
-        for t, raw, tile_ref in ((0, raw_r, own_r), (1, raw_g, own_g)):
-            owns[2 * t].wait()
-            value = raw[...]
-            blank = jnp.zeros((value.shape[0], 128 - tok), value.dtype)
-            tile_ref[...] = jnp.concatenate([value, blank], axis=1)
+        for copy in owns + loads:
+            copy.start()
         pl.semaphore_wait(barrier, xs - 1 + 2 * (nq - 1))
 
     info = ((own_r, xroutes, groutes), (own_g, xgates, ggates))
@@ -138,11 +131,17 @@
             si, sd = sends.take(), sends.take()
             for k in (2, 1, 3):
                 peer = (i + k) % xs
-                rdma(own, xinfo.at[i], si, x_sems[t][0], (peer, e)).start()
                 rdma(
                     part_of(data_refs[t], peer), xdata.at[t, i], sd, x_sems[t][1], (peer, e)
                 ).start()
+            raw = (raw_r, raw_g)[t]
+            owns[2 * t].wait()
+            value = raw[...]
+            blank = jnp.zeros((value.shape[0], 128 - tok), value.dtype)
+            own[...] = jnp.concatenate([value, blank], axis=1)
             xinfo[i] = own[...]
+            for k in (2, 1, 3):
+                rdma(own, xinfo.at[i], si, x_sems[t][0], ((i + k) % xs, e)).start()
             note_send(xinfo.at[pl.ds(0, xs - 1)], si)
             note_send(xdata.at[t, pl.ds(0, xs - 1)], sd)
 
@@ -641,7 +640,6 @@
     sem3 = back_open(1)
     with step("t_bk3own"):
         back_send(3, i, sem3)
-    do_cb(1)
     with step("t_wnear"):
         ring_near(dgu.at[3], g[3])
     with step("t_bk3lr"):
@@ -653,6 +651,7 @@
     with step("t_bk3opp"):
         back_send(3, opp, sem3)
         b[3] = [(ret.at[1, 3, others], sem3[1])]
+    do_cb(1)
     with step("t_ggu0"):
         grad_gate_up(0)
     do_cb(2)

time: 129 us -> 129 us (level)
  no operation moved by 1% of the time
where the time goes in v4:
time: 129 us
  Pallas kernels  128 us (99%)
    pallas_call x1, Pallas kernels, local(): pl.pallas_call(functools.partial(body, (n8, nc, dq, ff, tok)), out_shape=...  126 us

profile of v4, /device:TPU:1, one launch (start us, length us, event | category | flops | bytes accessed | tf_op | source)
XLA Modules:
  0.0 128.6 jit_solution(16546590137859988604)
XLA Ops:
  0.6 126.4 %moe_layer.1 = (bf16[16,2048]{1,0:T(8,128)(2,1)S(1)}, bf16[16,2048]{1,0:T(8,128)(2,1)S(1)}, bf16[1,512,768]{2,1,0:T(8,128)(2,1)S(1)}, bf16[1,512,768]{2,1,0:T(8,128)(2,1)S(1)}, bf16[1,768,512]{2,1,0:T(8,128)(2,1)S(1)}) custom-call(s32[8,16]{1,0:T(8,128)} %bitcast.11, f32[8,16]{1,0:T(8,128)} %bitcast.12, bf16[16,2048]{1,0:T(8,128)(2,1)} %tok_ref.1, ...), custom_call_target="tpu_custom_call" | custom-call | tf_op jit(solution)/shard_map/moe_layer/pallas_call | solution.py:720
  127.1 1.6 %hand_over.1 = (bf16[16,2048]{1,0:T(8,128)(2,1)}, bf16[16,2048]{1,0:T(8,128)(2,1)}, bf16[512,768]{1,0:T(8,128)(2,1)}, bf16[512,768]{1,0:T(8,128)(2,1)}, bf16[768,512]{1,0:T(8,128)(2,1)}) custom-call(bf16[16,2048]{1,0:T(8,128)(2,1)S(1)} %get-tuple-element.15.refs_0_, bf16[16,2048]{1,0:T(8,128)(2,1)S(1)} %get-tuple-element.16.refs_1_, ...), custom_call_target="tpu_custom_call" | custom-call | tf_op jit(solution)/shard_map/hand_over/pallas_call | solution.py:775
